TPU v7x, 32 devices: a whole 2x2x4 slice. The times are simulated.
32 devices in a mesh: parts: 2 (over y), seq: 4 (over z), head: 4 (over x, core).
Axes of the slice: x: 2, y: 2, z: 4, core: 2. Of those that a mesh axis runs over, the one named last changes fastest.
Arguments:
- xs: bfloat16 [8192, 5120], P(('parts', 'seq'), 'head'), parts along dimension 0, may hold values from -70 to 70
- gate_in: bfloat16 [8192, 5120], P(('parts', 'seq'), 'head'), parts along dimension 0, may hold values from -6 to 6
- bc_in: bfloat16 [8192, 256], P(('parts', 'seq')), parts along dimension 0, may hold values from -6 to 6
- dt_in: bfloat16 [8192, 64], P(('parts', 'seq'), 'head'), parts along dimension 0, may hold values from -3 to 3
- placement: int32 [8192], P(('parts', 'seq')), parts along dimension 0, may hold values from 0 to 4095, as said below
- lengths: int32 [6], P('parts'), parts along dimension 0, may hold values from 1 to 3072, 4096 in all
- conv_x: float32 [4, 5120], P(None, 'head'), may hold values from -3 to 3
- conv_bc: float32 [4, 256], replicated, may hold values from -3 to 3
- a_log: float32 [64], P('head'), may hold values from -9.5 to -0.5
- dt_bias: float32 [64], P('head'), may hold values from -3 to -1
- d_skip: float32 [64], P('head'), may hold values from 0.3 to 3
- norm_gain: float32 [5120], P('head'), may hold values from 0.1 to 1.9
Outputs:
- mixed: bfloat16 [8192, 5120], P(('parts', 'seq'), 'head'), parts along dimension 0
There are 2 independent parts, one for each index of `parts`. A program takes and returns all parts, laid end to end along the dimension named above; an argument that names none is the same for every part. Nothing has to cross between parts.
Inputs may be any that keep to these rules, and one draw needn't show every extreme that they name: `placement`: A permutation of the packed positions; each ingest device holds exactly 1024 // 4 rows bound for every sequence shard. The lengths sum to 4096; the longest is 3072.
All inputs are finite; a program needn't handle non-finite values.
Results may differ from a plain program's by a relative error of at most 0.0025.
The roundings to bfloat16 on the way count: a program that leaves them out, or rounds other values in their place, can miss the bound.
Values may be sent and summed in bfloat16 or wider, within the bound.
A program may use at most 128 MiB of HBM per device.

v0:
```python
import jax
import jax.numpy as jnp
from jax import lax
from jax.sharding import PartitionSpec as P

BLOCK = 256
INNER = 5120


highest = lax.Precision.HIGHEST


def passed_along(value, axis, steps):
    count = lax.axis_size(axis)
    first, last = (max(0, -steps), min(count, count - steps))
    return lax.ppermute(value, axis, [(source, source + steps) for source in range(first, last)])


def carried_in(array, axis, combine, identity):
    length, mine = (lax.axis_size(axis), lax.axis_index(axis))
    everything = jax.tree.map(lambda part: lax.all_gather(part, axis), array)
    start = jax.tree.map(
        lambda part, zero: jnp.broadcast_to(jnp.asarray(zero, part.dtype), part.shape),
        array,
        identity,
    )

    def step(k, before):
        reached = k < mine
        new = combine(before, jax.tree.map(lambda part: part[k], everything))
        return jax.tree.map(lambda a, b: jnp.where(reached, a, b), new, before)

    return lax.fori_loop(0, length, step, start)


def convolve(rows, docs_rows, kernel):
    width = kernel.shape[0]
    count = rows.shape[0] - (width - 1)
    total = jnp.zeros((count, rows.shape[1]), jnp.float32)
    for lag in range(width):
        lower = width - 1 - lag
        match = (docs_rows[lower : lower + count] == docs_rows[width - 1 :]).astype(jnp.float32)
        total = (
            total
            + kernel[lag][None, :]
            * rows[lower : lower + count].astype(jnp.float32)
            * match[:, None]
        )
    return jax.nn.silu(total).astype(jnp.bfloat16)


def block_pass(carry_state, pieces):
    conv_rows, key_rows, query_rows, step_sizes, log_decay, begins = pieces
    length = step_sizes.shape[0]
    head_count = step_sizes.shape[1]
    log_sums = jnp.cumsum(log_decay, axis=0)
    resets = jnp.cumsum(begins)
    places = jnp.arange(length)
    linked = (places[:, None] >= places[None, :]) & (resets[:, None] == resets[None, :])
    log_gaps = log_sums[:, None, :] - log_sums[None, :, :]
    weights = jnp.exp(jnp.where(linked[:, :, None], log_gaps, -jnp.inf))
    scores = jnp.dot(query_rows, key_rows.T, preferred_element_type=jnp.float32)
    mixing = scores[:, :, None] * weights * step_sizes[None, :, :]
    inputs = conv_rows.astype(jnp.float32).reshape(length, head_count, -1)
    outputs = jnp.einsum("tsh,shp->thp", mixing, inputs, precision=highest)
    carried = jnp.where((resets == 0)[:, None], jnp.exp(log_sums), 0.0)
    queries = query_rows.astype(jnp.float32)
    outputs = outputs + carried[:, :, None] * jnp.einsum(
        "tn,hpn->thp", queries, carry_state, precision=highest
    )
    closing = (
        jnp.where((resets == resets[-1])[:, None], jnp.exp(log_sums[-1][None, :] - log_sums), 0.0)
        * step_sizes
    )
    key_values = key_rows.astype(jnp.float32)
    carry_state = carried[-1][:, None, None] * carry_state + jnp.einsum(
        "sh,shp,sn->hpn", closing, inputs, key_values, precision=highest
    )
    return (carry_state, outputs.reshape(length, -1))


def link_states(earlier, later):
    early_log, early_reset, early_state = earlier
    late_log, late_reset, late_state = later
    keeping = jnp.where(late_reset > 0, 0.0, jnp.exp(late_log))
    return (
        early_log + late_log,
        jnp.maximum(early_reset, late_reset),
        keeping[:, None, None] * early_state + late_state,
    )


def body(
    xs,
    gate_in,
    bc_in,
    dt_in,
    placement,
    lengths,
    conv_x,
    conv_bc,
    a_log,
    dt_bias,
    d_skip,
    norm_gain,
):
    shards = lax.axis_size("seq")
    rows_dev = xs.shape[0]
    per_dest = rows_dev // shards
    targets = placement // rows_dev
    order = jnp.argsort(targets, stable=True)

    def grouped(array):
        return array[order].reshape((shards, per_dest) + array.shape[1:])

    arrived = (
        lax.all_to_all(grouped(xs), "seq", split_axis=0, concat_axis=0, tiled=True),
        lax.all_to_all(grouped(gate_in), "seq", split_axis=0, concat_axis=0, tiled=True),
        lax.all_to_all(grouped(bc_in), "seq", split_axis=0, concat_axis=0, tiled=True),
        lax.all_to_all(grouped(dt_in), "seq", split_axis=0, concat_axis=0, tiled=True),
    )
    slots = lax.all_to_all(grouped(placement), "seq", split_axis=0, concat_axis=0, tiled=True)
    local_slots = slots.reshape(-1) % rows_dev

    def settle(array):
        flat = array.reshape((rows_dev,) + array.shape[2:])
        return jnp.zeros_like(flat).at[local_slots].set(flat)

    packed_x = settle(arrived[0])
    packed_gate = settle(arrived[1])
    packed_bc = settle(arrived[2])
    packed_dt = settle(arrived[3])
    width = conv_x.shape[0]
    my_shard = lax.axis_index("seq")
    base = my_shard * rows_dev
    starts = jnp.cumsum(lengths) - lengths
    positions = base - (width - 1) + jnp.arange(rows_dev + width - 1, dtype=jnp.int32)
    docs = jnp.sum((starts[None, :] <= positions[:, None]).astype(jnp.int32), axis=1) - 1
    begins = jnp.sum((starts[None, :] == positions[width - 1 :, None]).astype(jnp.int32), axis=1)
    channels = jnp.concatenate([packed_x, packed_bc], 1)
    rim = passed_along(channels[rows_dev - width + 1 :], "seq", 1)
    convolved = convolve(
        jnp.concatenate([rim, channels], 0), docs, jnp.concatenate([conv_x, conv_bc], 1)
    )
    inner_dev = packed_x.shape[1]
    state_size = packed_bc.shape[1] // 2
    conv_rows = convolved[:, :inner_dev]
    key_rows = convolved[:, inner_dev : inner_dev + state_size]
    query_rows = convolved[:, inner_dev + state_size :]
    step_sizes = jax.nn.softplus(packed_dt.astype(jnp.float32) + dt_bias[None, :])
    log_decay = -jnp.exp(a_log)[None, :] * step_sizes
    head_count = step_sizes.shape[1]
    head_dim = inner_dev // head_count
    blocks = rows_dev // BLOCK

    def split(array):
        return array.reshape((blocks, BLOCK) + array.shape[1:])

    empty = jnp.zeros((head_count, head_dim, state_size), jnp.float32)
    local_state, outputs = lax.scan(
        block_pass,
        empty,
        (
            split(conv_rows),
            split(key_rows),
            split(query_rows),
            split(step_sizes),
            split(log_decay),
            split(begins),
        ),
    )
    outputs = outputs.reshape(rows_dev, head_count, head_dim)
    log_total = jnp.sum(log_decay, axis=0)
    reset_flag = jnp.broadcast_to((jnp.sum(begins) > 0).astype(jnp.float32), (head_count,))
    zero_heads = jnp.zeros((head_count,), jnp.float32)
    prefix = carried_in(
        (log_total, reset_flag, local_state), "seq", link_states, (zero_heads, zero_heads, empty)
    )
    incoming = prefix[2]
    shard_sums = jnp.cumsum(log_decay, axis=0)
    shard_resets = jnp.cumsum(begins)
    carried = jnp.where((shard_resets == 0)[:, None], jnp.exp(shard_sums), 0.0)
    queries = query_rows.astype(jnp.float32)
    outputs = outputs + carried[:, :, None] * jnp.einsum(
        "tn,hpn->thp", queries, incoming, precision=highest
    )
    inputs = conv_rows.astype(jnp.float32).reshape(rows_dev, head_count, head_dim)
    outputs = outputs + d_skip[None, :, None] * inputs
    gated = outputs.reshape(rows_dev, inner_dev) * jax.nn.silu(packed_gate.astype(jnp.float32))
    squares = lax.psum(jnp.sum(gated * gated, axis=1), "head")
    result = gated * lax.rsqrt(squares / INNER + 1e-05)[:, None] * norm_gain[None, :]
    return result.astype(jnp.bfloat16)


def solution(mesh):
    in_specs = (
        P(("parts", "seq"), "head"),
        P(("parts", "seq"), "head"),
        P(("parts", "seq"), None),
        P(("parts", "seq"), "head"),
        P(("parts", "seq")),
        P("parts"),
        P(None, "head"),
        P(),
        P("head"),
        P("head"),
        P("head"),
        P("head"),
    )
    out_specs = P(("parts", "seq"), "head")
    return jax.shard_map(body, mesh=mesh, in_specs=in_specs, out_specs=out_specs, check_vma=False)
```

profile of v0, /device:TPU:25, one launch (start us, length us, event | category | flops | bytes accessed | tf_op | source)
XLA Modules:
  0.0 477.7 jit_solution(12829732319555716730)
XLA Ops:
  7.4 4.4 sort.17
  11.8 10.4 %gather_fusion = s32[1024]{0:T(1024)} fusion(s32[1024]{0:T(1024)} %param.20, s32[1024]{0:T(1024)S(1)} %fusion.62), kind=kCustom, calls=%fused_computation | custom fusion | bytes 12288 | tf_op jit(solution)/shard_map/gather | solution.py:114
  22.2 4.5 all-to-all-start
  26.9 4.3 gather_fusion.1
  31.2 1.7 copy.103
  32.8 4.5 all-to-all-start.1
  37.4 4.9 %gather_fusion.3 = bf16[1024,256]{1,0:T(8,128)(2,1)} fusion(bf16[1024,256]{1,0:T(8,128)(2,1)S(1)} %copy-done.4, s32[1024]{0:T(1024)S(1)} %fusion.62), kind=kCustom, calls=%fused_computation.3 | custom fusion | bytes 1052672 | tf_op jit(solution)/shard_map/gather | solution.py:114
  42.3 4.5 all-to-all-start.3
  46.9 5.5 %gather_fusion.2 = bf16[1024,1280]{1,0:T(8,128)(2,1)} fusion(bf16[1024,1280]{1,0:T(8,128)(2,1)S(1)} %copy-done, s32[1024]{0:T(1024)S(1)} %fusion.62), kind=kCustom, calls=%fused_computation.2 | custom fusion | bytes 5246976 | tf_op jit(solution)/shard_map/gather | solution.py:114
  52.3 5.8 %all-to-all-done.3 = bf16[4,256,256]{2,1,0:T(8,128)(2,1)S(1)} async-done(((bf16[4,256,256]{2,1,0:T(8,128)(2,1)}), bf16[4,256,256]{2,1,0:T(8,128)(2,1)S(1)}, u32[]{:S(2)}, u32[]{:S(2)}) %all-to-all-start.3) | async-done | bytes 524320 | tf_op jit(solution)/shard_map/all_to_all | solution.py:119
  58.1 7.1 %all-to-all-start.2 = ((bf16[4,256,1280]{2,1,0:T(8,128)(2,1)}), bf16[4,256,1280]{2,1,0:T(8,128)(2,1)}, u32[]{:S(2)}, u32[]{:S(2)}) async-start(bf16[4,256,1280]{2,1,0:T(8,128)(2,1)} %bitcast.153), calls=%async_computation.2 | async-start | bytes 5242880 | tf_op jit(solution)/shard_map/all_to_all | solution.py:117
  66.9 5.5 %gather_fusion.4 = bf16[1024,1280]{1,0:T(8,128)(2,1)} fusion(bf16[1024,1280]{1,0:T(8,128)(2,1)S(1)} %copy-done.2, s32[1024]{0:T(1024)S(1)} %fusion.62), kind=kCustom, calls=%fused_computation.4 | custom fusion | bytes 5246976 | tf_op jit(solution)/shard_map/gather | solution.py:114
  72.9 3.2 scatter_custom_fusion
  76.3 6.1 %scatter_custom_fusion.2 = bf16[1024,256]{1,0:T(8,128)(2,1)} fusion(s32[1024]{0:T(1024)S(1)} %bitcast.170, bf16[1024,256]{1,0:T(8,128)(2,1)} %bitcast.160, bf16[]{:T(256)} %constant.117.clone.1), kind=kCustom, calls=%fused_computation.94 | custom fusion | bytes 524800 | tf_op jit(solution)/shard_map/scatter | solution.py:127
  82.4 38.9 %all-to-all-done.2 = bf16[4,256,1280]{2,1,0:T(8,128)(2,1)} async-done(((bf16[4,256,1280]{2,1,0:T(8,128)(2,1)}), bf16[4,256,1280]{2,1,0:T(8,128)(2,1)}, u32[]{:S(2)}, u32[]{:S(2)}) %all-to-all-start.2) | async-done | bytes 2621472 | tf_op jit(solution)/shard_map/all_to_all | solution.py:117
  121.3 7.6 %all-to-all-start.4 = ((bf16[4,256,1280]{2,1,0:T(8,128)(2,1)}), bf16[4,256,1280]{2,1,0:T(8,128)(2,1)}, u32[]{:S(2)}, u32[]{:S(2)}) async-start(bf16[4,256,1280]{2,1,0:T(8,128)(2,1)} %bitcast.152), calls=%async_computation.4 | async-start | bytes 5242880 | tf_op jit(solution)/shard_map/all_to_all | solution.py:118
  128.9 6.9 %scatter_custom_fusion.1 = bf16[1024,1280]{1,0:T(8,128)(2,1)S(1)} fusion(s32[1024]{0:T(1024)S(1)} %bitcast.171, bf16[1024,1280]{1,0:T(8,128)(2,1)} %bitcast.8, bf16[]{:T(256)} %constant.117.clone.1), kind=kCustom, calls=%fused_computation.90 | custom fusion | bytes 2621952 | tf_op jit(solution)/shard_map/scatter | solution.py:127
  137.0 1.7 copy-done.8
  138.7 1.5 collective-permute-start
  141.0 3.4 collective-permute-done
  144.4 10.6 %multiply_convert_fusion = bf16[1024,1536]{1,0:T(8,128)(2,1)S(1)} fusion(bf16[1024,1536]{1,0:T(8,128)(2,1)} %copy-done.8, bf16[3,1536]{1,0:T(4,128)(2,1)S(1)} %collective-permute-done, f32[1024]{0:T(1024)S(1)} %get-tuple-element.334, f32[1536]{0:T(1024)S(1)} %get-tuple-element.282, f32[1024]{0:T(1024)S(1)} %get-tuple-element.333, ...), kind=kLoop, calls=%fused_computation.75 | loop fusion | flops 44040192 | bytes 6337536 | tf_op jit(solution)/shard_map/convert_element_type | solution.py:49
  155.0 3.9 fusion.72
  159.1 179.0 %while.27 = (s32[]{:T(128)}, f32[16,80,128]{2,1,0:T(8,128)S(1)}, f32[4,256,1280]{1,0,2:T(4,128)}, s32[4,256]{1,0:T(4,128)}, f32[4,256,16]{1,0,2:T(4,128)S(1)}, /...) while((s32[]{:T(128)}, f32[16,80,128]{2,1,0:T(8,128)S(1)}, ...), condition=%wide.region_12.13_spmd.clone, body=%wide.region_7.12_spmd.clone.sunk | while | flops 2036978176 | bytes 17380640 | solution.py:160
  163.1 3.2 fusion.101
  169.7 5.4 %copy.156 = f32[1,256,1280]{1,0,2:T(1,128)S(1)} copy(f32[1,256,1280]{1,2,0:T(8,128)S(1)} %bitcast.146) | data formatting | bytes 2621440 | tf_op jit(solution)/shard_map/while/body/jit(dynamic_update_index_in_dim)/dynamic_update_slice | solution.py:160
  175.2 28.6 %dynamic_update_slice.6 = f32[4,256,1280]{1,0,2:T(4,128)} dynamic-update-slice(f32[4,256,1280]{1,0,2:T(4,128)} %get-tuple-element.453, f32[1,256,1280]{1,0,2:T(1,128)S(1)} %copy.156, s32[]{:T(128)S(6)} %copy.163, s32[]{:T(128)} %constant.115.clone.1..sunk, s32[]{:T(128)} %constant.115.clone.1..sunk) | dynamic-update-slice | bytes 2621444 | tf_op jit(solution)/shard_map/while/body/jit(dynamic_update_index_in_dim)/dynamic_update_slice | solution.py:160
  207.8 3.2 fusion.101
  214.5 5.4 %copy.156 = f32[1,256,1280]{1,0,2:T(1,128)S(1)} copy(f32[1,256,1280]{1,2,0:T(8,128)S(1)} %bitcast.146) | data formatting | bytes 2621440 | tf_op jit(solution)/shard_map/while/body/jit(dynamic_update_index_in_dim)/dynamic_update_slice | solution.py:160
  219.9 28.6 %dynamic_update_slice.6 = f32[4,256,1280]{1,0,2:T(4,128)} dynamic-update-slice(f32[4,256,1280]{1,0,2:T(4,128)} %get-tuple-element.453, f32[1,256,1280]{1,0,2:T(1,128)S(1)} %copy.156, s32[]{:T(128)S(6)} %copy.163, s32[]{:T(128)} %constant.115.clone.1..sunk, s32[]{:T(128)} %constant.115.clone.1..sunk) | dynamic-update-slice | bytes 2621444 | tf_op jit(solution)/shard_map/while/body/jit(dynamic_update_index_in_dim)/dynamic_update_slice | solution.py:160
  252.6 3.2 fusion.101
  259.2 5.4 %copy.156 = f32[1,256,1280]{1,0,2:T(1,128)S(1)} copy(f32[1,256,1280]{1,2,0:T(8,128)S(1)} %bitcast.146) | data formatting | bytes 2621440 | tf_op jit(solution)/shard_map/while/body/jit(dynamic_update_index_in_dim)/dynamic_update_slice | solution.py:160
  264.7 28.6 %dynamic_update_slice.6 = f32[4,256,1280]{1,0,2:T(4,128)} dynamic-update-slice(f32[4,256,1280]{1,0,2:T(4,128)} %get-tuple-element.453, f32[1,256,1280]{1,0,2:T(1,128)S(1)} %copy.156, s32[]{:T(128)S(6)} %copy.163, s32[]{:T(128)} %constant.115.clone.1..sunk, s32[]{:T(128)} %constant.115.clone.1..sunk) | dynamic-update-slice | bytes 2621444 | tf_op jit(solution)/shard_map/while/body/jit(dynamic_update_index_in_dim)/dynamic_update_slice | solution.py:160
  297.3 3.2 fusion.101
  304.0 5.4 %copy.156 = f32[1,256,1280]{1,0,2:T(1,128)S(1)} copy(f32[1,256,1280]{1,2,0:T(8,128)S(1)} %bitcast.146) | data formatting | bytes 2621440 | tf_op jit(solution)/shard_map/while/body/jit(dynamic_update_index_in_dim)/dynamic_update_slice | solution.py:160
  309.4 28.6 %dynamic_update_slice.6 = f32[4,256,1280]{1,0,2:T(4,128)} dynamic-update-slice(f32[4,256,1280]{1,0,2:T(4,128)} %get-tuple-element.453, f32[1,256,1280]{1,0,2:T(1,128)S(1)} %copy.156, s32[]{:T(128)S(6)} %copy.163, s32[]{:T(128)} %constant.115.clone.1..sunk, s32[]{:T(128)} %constant.115.clone.1..sunk) | dynamic-update-slice | bytes 2621444 | tf_op jit(solution)/shard_map/while/body/jit(dynamic_update_index_in_dim)/dynamic_update_slice | solution.py:160
  344.3 46.1 %all-reduce.2 = (f32[4]{0:T(128)S(1)}, f32[64]{0:T(128)S(1)}) all-reduce(f32[4]{0:T(128)S(1)} %dynamic-update-slice, f32[64]{0:T(128)S(1)} %dynamic-update-slice.1), channel_id=2, replica_groups=mesh['parts'=2,'seq'=4,'head'=4] {'seq'}, use_global_device_ids=true, to_apply=%add | all-reduce | flops 68 | bytes 544
  391.4 4.5 reduce-window.54
  396.4 7.0 %scatter_custom_fusion.3 = bf16[1024,1280]{1,0:T(8,128)(2,1)S(1)} fusion(s32[1024]{0:T(1024)} %bitcast.172, bf16[1024,1280]{1,0:T(8,128)(2,1)} %bitcast.27, bf16[]{:T(256)} %constant.117.clone.1), kind=kCustom, calls=%fused_computation.88 | custom fusion | bytes 2621952 | tf_op jit(solution)/shard_map/scatter | solution.py:127
  403.4 7.0 %copy.113 = f32[1024,1280]{0,1:T(8,128)} copy(f32[1024,1280]{1,0:T(8,128)} %get-tuple-element.330) | data formatting | bytes 10485760 | tf_op jit(solution)/shard_map/reshape | solution.py:187
  410.4 7.7 %reshape.351 = f32[1024,16,80]{0,2,1:T(8,128)} reshape(f32[4,256,1280]{1,0,2:T(4,128)} %get-tuple-element.164) | data formatting | bytes 10485760 | tf_op jit(solution)/shard_map/reshape | solution.py:172
  418.1 15.9 %all-gather.4.cloned.1.call-done = f32[64,80,128]{2,1,0:T(8,128)} async-done(((f32[16,80,128]{2,1,0:T(8,128)}), f32[64,80,128]{2,1,0:T(8,128)}) %all-gather.4.cloned.1.call-update) | async-done | bytes 2621456 | tf_op jit(solution)/shard_map/all_gather | solution.py:21
  434.1 5.1 %while.28 = (s32[]{:T(128)}, f32[16,80,128]{2,1,0:T(8,128)S(1)}, s32[]{:T(128)}, f32[4,16]{1,0:T(4,128)S(1)}, f32[4,16]{1,0:T(4,128)S(1)}, /*index=5*/f32[4,16,80,128]{3,2,1,0:T(8,128)}, s32[]{:T(128)}, s32[]{:T(128)}) while((s32[]{:T(128)}, f32[16,80,128]{2,1,0:T(8,128)S(1)}, s32[]{:T(128)}, f32[4,16]{1,0:T(4,128)S(1)}, ...), condition=%wide.region_20.21_spmd.clone, body=%wide.region_19.20_spmd.clone.sunk | while | flops 655396 | bytes 1966457 | solution.py:33
  439.2 3.3 fusion.54
  442.5 6.9 %multiply_add_fusion = f32[1024,16,80]{0,2,1:T(8,128)} fusion(f32[1024,16,80]{0,2,1:T(8,128)} %bitcast.149, f32[1024,16,80]{0,2,1:T(8,128)S(1)} %copy-done.6, f32[1024,16,80]{0,2,1:T(8,128)S(1)} %fusion.54, f32[16]{0:T(128)S(1)} %copy-done.25, f32[1024,16]{0,1:T(8,128)S(1)} %fusion.60), kind=kLoop, calls=%fused_computation.82 | loop fusion | flops 5242880 | bytes 21037120 | tf_op jit(solution)/shard_map/add | solution.py:188
  449.4 6.0 %copy.114 = f32[1024,1280]{1,0:T(8,128)} copy(f32[1024,1280]{0,1:T(8,128)} %bitcast.150) | data formatting | bytes 10485760 | tf_op jit(solution)/shard_map/reshape | solution.py:189
  455.4 4.2 multiply_reduce_fusion
  459.6 5.6 %psum.7 = f32[1024]{0:T(1024)S(1)} all-reduce(f32[1024]{0:T(1024)S(1)} %multiply_reduce_fusion), channel_id=1, replica_groups=mesh['parts'=2,'seq'=4,'head'=4] {'head'}, use_global_device_ids=true, to_apply=%region_23.24 | all-reduce | flops 1024 | bytes 8192 | tf_op jit(solution)/shard_map/psum | solution.py:190
  465.2 5.7 %multiply_convert_fusion.1 = bf16[1024,1280]{1,0:T(8,128)(2,1)} fusion(f32[1280]{0:T(1024)S(1)} %copy-done.21, f32[1024]{0:T(1024)S(1)} %add_rsqrt_fusion, f32[1024,1280]{1,0:T(8,128)} %copy.114, bf16[1024,1280]{1,0:T(8,128)(2,1)} %copy-done.5), kind=kLoop, calls=%fused_computation.80 | loop fusion | flops 11796480 | bytes 10494976 | tf_op jit(solution)/shard_map/convert_element_type | solution.py:192
  (255 shorter events, 46.3 us)
Async XLA Ops:
  6.5 40.3 %copy-start = (bf16[1024,1280]{1,0:T(8,128)(2,1)S(1)}, bf16[1024,1280]{1,0:T(8,128)(2,1)}, u32[]{:S(2)}) copy-start(bf16[1024,1280]{1,0:T(8,128)(2,1)} %param.16) | copy-start | bytes 7864324
  6.5 20.2 %copy-start.19 = (bf16[1024,16]{0,1:T(8,128)(2,1)S(1)}, bf16[1024,16]{0,1:T(8,128)(2,1)}, u32[]{:S(2)}) copy-start(bf16[1024,16]{0,1:T(8,128)(2,1)} %param.19) | copy-start | bytes 98308
  6.5 30.8 %copy-start.4 = (bf16[1024,256]{1,0:T(8,128)(2,1)S(1)}, bf16[1024,256]{1,0:T(8,128)(2,1)}, u32[]{:S(2)}) copy-start(bf16[1024,256]{1,0:T(8,128)(2,1)} %param.18) | copy-start | bytes 1572868
  22.2 10.7 %all-to-all-start = ((s32[4,1,256]{2,1,0:T(1,128)}), s32[4,1,256]{2,1,0:T(1,128)S(1)}, u32[]{:S(2)}, u32[]{:S(2)}) async-start(s32[4,1,256]{2,1,0:T(1,128)} %bitcast.2), calls=%async_computation | async-start | bytes 8192 | tf_op jit(solution)/shard_map/all_to_all | solution.py:122
  32.8 9.5 %all-to-all-start.1 = ((bf16[4,256,16]{1,2,0:T(8,128)(2,1)}), bf16[4,256,16]{1,2,0:T(8,128)(2,1)S(1)}, u32[]{:S(2)}, u32[]{:S(2)}) async-start(bf16[4,256,16]{1,2,0:T(8,128)(2,1)} %copy.103), calls=%async_computation.1 | async-start | bytes 65536 | tf_op jit(solution)/shard_map/all_to_all | solution.py:120
  42.3 15.8 %all-to-all-start.3 = ((bf16[4,256,256]{2,1,0:T(8,128)(2,1)}), bf16[4,256,256]{2,1,0:T(8,128)(2,1)S(1)}, u32[]{:S(2)}, u32[]{:S(2)}) async-start(bf16[4,256,256]{2,1,0:T(8,128)(2,1)} %bitcast.157), calls=%async_computation.3 | async-start | bytes 1048576 | tf_op jit(solution)/shard_map/all_to_all | solution.py:119
  52.3 13.0 %copy-start.26 = (s32[3]{0:T(128)S(1)}, s32[3]{0:T(128)}, u32[]{:S(2)}) copy-start(s32[3]{0:T(128)} %param.21) | copy-start | bytes 40
  52.3 14.6 %copy-start.2 = (bf16[1024,1280]{1,0:T(8,128)(2,1)S(1)}, bf16[1024,1280]{1,0:T(8,128)(2,1)}, u32[]{:S(2)}) copy-start(bf16[1024,1280]{1,0:T(8,128)(2,1)} %param.17) | copy-start | bytes 7864324
  58.1 7.2 %copy-start.11 = (bf16[4,256,256]{2,1,0:T(8,128)(2,1)}, bf16[4,256,256]{2,1,0:T(8,128)(2,1)S(1)}, u32[]{:S(2)}) copy-start(bf16[4,256,256]{2,1,0:T(8,128)(2,1)S(1)} %all-to-all-done.3) | copy-start | bytes 1572868
  58.1 63.2 %all-to-all-start.2 = ((bf16[4,256,1280]{2,1,0:T(8,128)(2,1)}), bf16[4,256,1280]{2,1,0:T(8,128)(2,1)}, u32[]{:S(2)}, u32[]{:S(2)}) async-start(bf16[4,256,1280]{2,1,0:T(8,128)(2,1)} %bitcast.153), calls=%async_computation.2 | async-start | bytes 5242880 | tf_op jit(solution)/shard_map/all_to_all | solution.py:117
  66.3 6.1 %copy-start.18 = (s32[1024]{0:T(1024)}, s32[1024]{0:T(1024)S(1)}, u32[]{:S(2)}) copy-start(s32[1024]{0:T(1024)S(1)} %get-tuple-element.286) | copy-start | bytes 12292
  66.9 5.5 %copy-start.20 = (f32[4,1280]{1,0:T(4,128)S(1)}, f32[4,1280]{1,0:T(4,128)}, u32[]{:S(2)}) copy-start(f32[4,1280]{1,0:T(4,128)} %param.22) | copy-start | bytes 61444
  66.9 5.5 %copy-start.22 = (f32[4,256]{1,0:T(4,128)S(1)}, f32[4,256]{1,0:T(4,128)}, u32[]{:S(2)}) copy-start(f32[4,256]{1,0:T(4,128)} %param.23) | copy-start | bytes 12292
  66.9 5.7 %copy-start.27 = (f32[16]{0:T(128)S(1)}, f32[16]{0:T(128)}, u32[]{:S(2)}) copy-start(f32[16]{0:T(128)} %param.24) | copy-start | bytes 196
  72.7 63.1 %copy-start.23 = (s32[1024,1]{0,1:T(1,128)}, s32[1024,1]{0,1:T(1,128)S(1)}, u32[]{:S(2)}) copy-start(s32[1024,1]{0,1:T(1,128)S(1)} %compare_select_fusion.2) | copy-start | bytes 12292
  121.3 275.1 %all-to-all-start.4 = ((bf16[4,256,1280]{2,1,0:T(8,128)(2,1)}), bf16[4,256,1280]{2,1,0:T(8,128)(2,1)}, u32[]{:S(2)}, u32[]{:S(2)}) async-start(bf16[4,256,1280]{2,1,0:T(8,128)(2,1)} %bitcast.152), calls=%async_computation.4 | async-start | bytes 5242880 | tf_op jit(solution)/shard_map/all_to_all | solution.py:118
  128.9 305.1 %all-gather.4.cloned.1.call-start = ((), (), s32[]{:S(2)}) async-start(), calls=%async_computation.5 | async-start | bytes 3276800 | tf_op jit(solution)/shard_map/all_gather | solution.py:21
  128.9 11.2 %copy-start.24 = (f32[16]{0:T(128)S(1)}, f32[16]{0:T(128)}, u32[]{:S(2)}) copy-start(f32[16]{0:T(128)} %param.25) | copy-start | bytes 196
  137.0 1.7 copy-start.8
  138.7 5.7 %collective-permute-start = (bf16[3,1536]{1,0:T(4,128)(2,1)S(1)}, bf16[3,1536]{1,0:T(4,128)(2,1)S(1)}, u32[]{:S(2)}, u32[]{:S(2)}) collective-permute-start(bf16[3,1536]{1,0:T(4,128)(2,1)S(1)} %slice.130), channel_id=1, source_target_pairs={{0,4},{4,8},{8,12},{1,5},{5,9},{9,13},{2,6},{6,10},{10,14},{3,7},{... | collective-permute-start | bytes 27656 | tf_op jit(solution)/shard_map/ppermute | solution.py:16
  141.0 17.9 %copy-start.10 = (f32[1024,16]{0,1:T(8,128)}, f32[1024,16]{0,1:T(8,128)S(1)}, u32[]{:S(2)}) copy-start(f32[1024,16]{0,1:T(8,128)S(1)} %get-tuple-element.322) | copy-start | bytes 196612
  155.0 4.0 copy-start.7
  159.1 2.3 copy-start.12
  159.1 3.9 copy-start.14
  161.4 1.6 copy-start.16
  162.9 4.7 copy-start.17
  168.5 35.3 %copy-start.13 = (f32[4,256,16]{1,0,2:T(4,128)S(1)}, f32[4,256,16]{1,0,2:T(4,128)}, u32[]{:S(2)}) copy-start(f32[4,256,16]{1,0,2:T(4,128)} %copy-done.12) | copy-start | bytes 196612 | tf_op jit(solution)/shard_map/while
  168.5 35.3 %copy-start.15 = (f32[4,256,16]{1,0,2:T(4,128)S(1)}, f32[4,256,16]{1,0,2:T(4,128)}, u32[]{:S(2)}) copy-start(f32[4,256,16]{1,0,2:T(4,128)} %copy-done.14) | copy-start | bytes 196612 | tf_op jit(solution)/shard_map/while
  203.8 2.3 copy-start.12
  203.8 3.9 copy-start.14
  207.7 4.7 copy-start.17
  213.2 35.3 %copy-start.13 = (f32[4,256,16]{1,0,2:T(4,128)S(1)}, f32[4,256,16]{1,0,2:T(4,128)}, u32[]{:S(2)}) copy-start(f32[4,256,16]{1,0,2:T(4,128)} %copy-done.12) | copy-start | bytes 196612 | tf_op jit(solution)/shard_map/while
  213.3 35.3 %copy-start.15 = (f32[4,256,16]{1,0,2:T(4,128)S(1)}, f32[4,256,16]{1,0,2:T(4,128)}, u32[]{:S(2)}) copy-start(f32[4,256,16]{1,0,2:T(4,128)} %copy-done.14) | copy-start | bytes 196612 | tf_op jit(solution)/shard_map/while
  248.6 2.3 copy-start.12
  248.6 3.9 copy-start.14
  252.4 4.7 copy-start.17
  258.0 35.3 %copy-start.13 = (f32[4,256,16]{1,0,2:T(4,128)S(1)}, f32[4,256,16]{1,0,2:T(4,128)}, u32[]{:S(2)}) copy-start(f32[4,256,16]{1,0,2:T(4,128)} %copy-done.12) | copy-start | bytes 196612 | tf_op jit(solution)/shard_map/while
  258.0 35.3 %copy-start.15 = (f32[4,256,16]{1,0,2:T(4,128)S(1)}, f32[4,256,16]{1,0,2:T(4,128)}, u32[]{:S(2)}) copy-start(f32[4,256,16]{1,0,2:T(4,128)} %copy-done.14) | copy-start | bytes 196612 | tf_op jit(solution)/shard_map/while
  293.3 2.3 copy-start.12
  293.3 3.9 copy-start.14
  297.2 4.7 copy-start.17
  302.7 35.3 %copy-start.13 = (f32[4,256,16]{1,0,2:T(4,128)S(1)}, f32[4,256,16]{1,0,2:T(4,128)}, u32[]{:S(2)}) copy-start(f32[4,256,16]{1,0,2:T(4,128)} %copy-done.12) | copy-start | bytes 196612 | tf_op jit(solution)/shard_map/while
  302.8 35.3 %copy-start.15 = (f32[4,256,16]{1,0,2:T(4,128)S(1)}, f32[4,256,16]{1,0,2:T(4,128)}, u32[]{:S(2)}) copy-start(f32[4,256,16]{1,0,2:T(4,128)} %copy-done.14) | copy-start | bytes 196612 | tf_op jit(solution)/shard_map/while
  403.4 52.0 %copy-start.5 = (bf16[1024,1280]{1,0:T(8,128)(2,1)}, bf16[1024,1280]{1,0:T(8,128)(2,1)S(1)}, u32[]{:S(2)}) copy-start(bf16[1024,1280]{1,0:T(8,128)(2,1)S(1)} %scatter_custom_fusion.3) | copy-start | bytes 7864324
  439.2 3.3 copy-start.6
  439.2 3.3 copy-start.25
  455.4 9.8 %copy-start.21 = (f32[1280]{0:T(1024)S(1)}, f32[1280]{0:T(1024)}, u32[]{:S(2)}) copy-start(f32[1280]{0:T(1024)} %param.27) | copy-start | bytes 15364
  465.2 5.7 %copy-start.1 = (bf16[1024,1280]{1,0:T(8,128)(2,1)S(1)}, bf16[1024,1280]{1,0:T(8,128)(2,1)}, u32[]{:S(2)}) copy-start(bf16[1024,1280]{1,0:T(8,128)(2,1)} %param.16) | copy-start | bytes 7864324
  (5 other events, 6.6 us)
Sparse Core Ops, SparseCore 0:
  339.1 94.9 all-gather.3
where the time goes:
time: 487 us; the launch traced here: 478 us
  local copies, waits for them, and re-layouts  236 us (48%)
  waiting for transfers between devices  64.1 us (13%)
  other arithmetic  56.9 us (12%)
  blocking collectives  51.7 us (11%)
  starting transfers between devices  29.8 us (6%)
  matrix products  23.7 us (5%)
  between operations  15 us (3%)
    dynamic_update_slice x8, local copies, waits for them, and re-layouts, body(): lax.scan(block_pass, empty, (split(conv_rows), split(key_rows), split(que...  136 us
    unnamed x1, blocking collectives  46.1 us
    all_to_all x1, waiting for transfers between devices, body(): lax.all_to_all(grouped(xs), 'seq', split_axis=0, concat_axis=0, tiled=True)  38.9 us
    gather x5, local copies, waits for them, and re-layouts, grouped(): return array[order].reshape((shards, per_dest) + array.shape[1:])  30.6 us
    scatter x5, local copies, waits for them, and re-layouts, settle(): return jnp.zeros_like(flat).at[local_slots].set(flat)  23.4 us
    all_gather x1, waiting for transfers between devices, carried_in(): everything = jax.tree.map(lambda part: lax.all_gather(part, axis), array)  15.9 us
    dot_general x4, matrix products, block_pass(): outputs = jnp.einsum('tsh,shp->thp', mixing, inputs, precision=highest)  12.7 us
    convert_element_type x1, other arithmetic, convolve(): return jax.nn.silu(total).astype(jnp.bfloat16)  10.6 us
  transfers between devices with their start and end apart: 7, of which 4 were waited for; matrix products, arithmetic and copies ran while one was open for 56% of the time, Pallas kernels for 0%

commit v1 on v0

v1 whole, which is shorter than its diff:
```python
import functools

import jax
import jax.numpy as jnp
from jax import lax
from jax.experimental import pallas as pl
from jax.experimental.pallas import tpu as pltpu
from jax.sharding import PartitionSpec as P

BLOCK = 256
LANES = 128
RIM = 8
HIGHEST = lax.Precision.HIGHEST
F32 = jnp.float32
BF16 = jnp.bfloat16


def iota(shape, dim):
    return lax.broadcasted_iota(jnp.int32, shape, dim)


def dot(a, b, dims=((1,), (0,))):
    return lax.dot_general(a, b, (dims, ((), ())), preferred_element_type=F32)


def halves(value):
    high = value.astype(BF16)
    return high, (value - high.astype(F32)).astype(BF16)


def dot_left(a, b):
    high, low = halves(a)
    return dot(high, b) + dot(low, b)


def dot_right(a, b, dims=((1,), (0,))):
    high, low = halves(b)
    return dot(a, high, dims) + dot(a, low, dims)


def spread(head_dim, width):
    head, channel = iota((LANES, width), 0), iota((LANES, width), 1)
    inside = (channel >= head * head_dim) & (channel < (head + 1) * head_dim)
    return inside.astype(F32).astype(BF16)


def send_kernel(shards, per, rim, width, place_ref, *refs):
    ins, (out_ref, slot_ref) = refs[:-2], refs[-2:]
    rows = place_ref.shape[1]
    dest = pl.program_id(0)
    place = place_ref[0:1, :]
    target = lax.shift_right_logical(place, rows.bit_length() - 1)

    @pl.when(dest == 0)
    def _():
        groups = -(-shards // 16) * 16
        chosen = iota((groups, rows), 0) == target
        before = (iota((rows, rows), 0) < iota((rows, rows), 1)).astype(F32).astype(BF16)
        counts = dot(chosen.astype(F32).astype(BF16), before)
        slot = jnp.sum(jnp.where(chosen, counts, 0.0), axis=0, keepdims=True)
        slot_ref[...] = jnp.broadcast_to(slot.astype(jnp.int32), slot_ref.shape)

    offset = place - dest * rows
    key = jnp.where(target == dest, slot_ref[0:1, :], -1)
    if rim:
        key = jnp.where((offset < 0) & (offset >= 1 - width), offset + (width - 1 + per), key)
    pick = (iota((per + rim, rows), 0) == key).astype(F32).astype(BF16)
    column = 0
    for ref in ins:
        count = ref.shape[1]
        out_ref[0, :, column : column + count] = dot(pick, ref[...]).astype(BF16)
        column += count


def send_rows(place, arrays, shards, rim, width):
    rows = place.shape[1]
    per = rows // shards
    columns = sum(array.shape[1] for array in arrays)
    return pl.pallas_call(
        functools.partial(send_kernel, shards, per, rim, width),
        grid=(shards,),
        in_specs=[pl.BlockSpec(place.shape, lambda k: (0, 0))]
        + [pl.BlockSpec(array.shape, lambda k: (0, 0)) for array in arrays],
        out_specs=pl.BlockSpec((1, per + rim, columns), lambda k: (k, 0, 0)),
        out_shape=jax.ShapeDtypeStruct((shards, per + rim, columns), BF16),
        scratch_shapes=[pltpu.VMEM((8, rows), jnp.int32)],
        cost_estimate=pl.CostEstimate(
            flops=2 * rows * rows * columns, bytes_accessed=4 * rows * columns, transcendentals=0
        ),
    )(place, *arrays)


def doc_at(start_ref, position):
    total = jnp.where(start_ref[0] <= position, 1, 0)
    for j in range(1, start_ref.shape[0] - 1):
        total = total + jnp.where(start_ref[j] <= position, 1, 0)
    return total


def scan_kernel(
    per, heads, start_ref, arrived_ref, taps_ref, head_ref, skip_ref,
    y_ref, query_ref, carry_ref, slot_ref, state_ref, total_ref,
):
    chunk = pl.program_id(0)
    width = taps_ref.shape[0]
    inner = y_ref.shape[1]
    head_dim = inner // heads
    mixed = inner + 2 * LANES
    rows_in = arrived_ref.shape[0]
    base = start_ref[start_ref.shape[0] - 1]
    origin = base + chunk * BLOCK

    @pl.when(chunk == 0)
    def _():
        tail = arrived_ref[:, mixed : mixed + LANES]
        lane, row = iota((16, LANES), 1), iota((16, LANES), 0)
        factor = jnp.where(lane == heads, 32.0, jnp.where(lane == heads + 1, 1.0, 0.0))
        factor = jnp.where(row == 0, factor, 0.0).astype(BF16)
        place = dot(factor, tail, ((1,), (1,)))[0:8, :].astype(jnp.int32)
        within = iota((8, rows_in), 1) % (per + RIM)
        slot_ref[...] = jnp.where(within >= per, place - pl.num_programs(0) * BLOCK, place)
        state_ref[...] = jnp.zeros_like(state_ref)
        total_ref[...] = jnp.zeros_like(total_ref)

    wanted = iota((BLOCK + RIM, rows_in), 0) + (chunk * BLOCK - RIM)
    pick = (wanted == slot_ref[0:1, :]).astype(F32).astype(BF16)
    column = iota((BLOCK, 1), 0) + origin
    docs = doc_at(start_ref, column)
    matches = [None] + [
        (doc_at(start_ref, column - lag) == docs) & (column >= lag) for lag in range(1, width)
    ]

    def convolved(first, count):
        packed = dot(pick, arrived_ref[:, first : first + count])
        total = taps_ref[0:1, first : first + count] * packed[RIM:, :]
        for lag in range(1, width):
            part = taps_ref[lag : lag + 1, first : first + count] * packed[RIM - lag : RIM - lag + BLOCK, :]
            total = total + jnp.where(matches[lag], part, 0.0)
        return (total * jax.nn.sigmoid(total)).astype(BF16)

    x = convolved(0, inner)
    keys = convolved(inner, LANES)
    query = convolved(inner + LANES, LANES)
    query_ref[...] = query
    raw = dot(pick, arrived_ref[:, mixed : mixed + LANES])[RIM:, :]
    raw = raw + head_ref[1:2, :]
    lane = iota((1, LANES), 1)
    step = jnp.maximum(raw, 0.0) + jnp.log1p(jnp.exp(-jnp.abs(raw)))
    step = jnp.where(lane < heads, step, 0.0)
    rate = jnp.exp(head_ref[0:1, :])
    decay = -rate * step
    lower = iota((BLOCK, BLOCK), 0) >= iota((BLOCK, BLOCK), 1)
    sums = jnp.dot(lower.astype(F32), decay, precision=HIGHEST, preferred_element_type=F32)
    sums_t = sums.T
    step_t = step.T
    docs_row = doc_at(start_ref, iota((1, BLOCK), 1) + origin)
    linked = lower & (docs == docs_row)
    scores = jnp.where(linked, dot(query, keys, ((1,), (1,))), 0.0)
    doc_before = doc_at(start_ref, origin - 1)
    doc_before = jnp.where(origin > 0, doc_before, 0)
    doc_base = jnp.where(base > 0, doc_at(start_ref, base - 1), 0)
    doc_last = doc_at(start_ref, origin + BLOCK - 1)
    carried = jnp.where(docs == doc_before, jnp.exp(sums), 0.0)
    last = sums[BLOCK - 1 : BLOCK, :]
    closing = jnp.where(docs == doc_last, jnp.exp(jnp.minimum(last - sums, 0.0)), 0.0) * step
    before = total_ref[0:1, :]
    carry_ref[...] = jnp.where(docs == doc_base, jnp.exp(before + sums), 0.0)
    total_ref[...] = jnp.broadcast_to(before + last, total_ref.shape)

    expand = spread(head_dim, inner)
    carried_all = dot_left(carried, expand)
    state = state_ref[...]
    x32 = x.astype(F32)
    y_ref[...] = carried_all * dot_right(query, state) + skip_ref[0:1, :] * x32
    weighted = dot_left(closing, expand) * x32
    state_ref[...] = carried_all[BLOCK - 1 : BLOCK, :] * state + dot_right(keys, weighted, ((0,), (0,)))

    for head in range(heads):
        first, end = head * head_dim, (head + 1) * head_dim
        low, high = first // LANES * LANES, -(-end // LANES) * LANES
        gap = sums[:, head : head + 1] - sums_t[head : head + 1, :]
        weight = jnp.exp(jnp.minimum(gap, 0.0)) * step_t[head : head + 1, :] * scores
        channel = iota((1, high - low), 1) + low
        own = jnp.where((channel >= first) & (channel < end), x32[:, low:high], 0.0).astype(BF16)
        y_ref[:, low:high] += dot_left(weight, own)


def scan_blocks(starts, arrived, taps, head_rows, skip, per, heads, rows):
    rows_in, columns = arrived.shape
    inner = skip.shape[1]
    fixed = lambda shape: pl.BlockSpec(shape, lambda c: (0, 0))
    return pl.pallas_call(
        functools.partial(scan_kernel, per, heads),
        grid=(rows // BLOCK,),
        in_specs=[
            pl.BlockSpec(memory_space=pltpu.SMEM),
            fixed(arrived.shape),
            fixed(taps.shape),
            fixed(head_rows.shape),
            fixed(skip.shape),
        ],
        out_specs=[
            pl.BlockSpec((BLOCK, inner), lambda c: (c, 0)),
            pl.BlockSpec((BLOCK, LANES), lambda c: (c, 0)),
            pl.BlockSpec((BLOCK, LANES), lambda c: (c, 0)),
            fixed((8, rows_in)),
            fixed((LANES, inner)),
        ],
        out_shape=[
            jax.ShapeDtypeStruct((rows, inner), F32),
            jax.ShapeDtypeStruct((rows, LANES), BF16),
            jax.ShapeDtypeStruct((rows, LANES), F32),
            jax.ShapeDtypeStruct((8, rows_in), jnp.int32),
            jax.ShapeDtypeStruct((LANES, inner), F32),
        ],
        scratch_shapes=[pltpu.VMEM((8, LANES), F32)],
        compiler_params=pltpu.CompilerParams(vmem_limit_bytes=56 << 20),
        cost_estimate=pl.CostEstimate(
            flops=20_000_000_000, bytes_accessed=12_000_000, transcendentals=rows * BLOCK * heads
        ),
    )(starts, arrived, taps, head_rows, skip)


def gate_kernel(heads, gate_ref, slot_ref, y_ref, query_ref, carry_ref, state_ref, out_ref, square_ref):
    chunk = pl.program_id(0)
    inner = y_ref.shape[1]
    rows_in = gate_ref.shape[0]
    pick = (iota((BLOCK, rows_in), 0) + chunk * BLOCK == slot_ref[0:1, :]).astype(F32).astype(BF16)
    gate = dot(pick, gate_ref[...])
    expand = spread(inner // heads, inner)
    y = y_ref[...] + dot_left(carry_ref[...], expand) * dot_right(query_ref[...], state_ref[...])
    gated = y * (gate * jax.nn.sigmoid(gate))
    out_ref[...] = gated
    squares = jnp.sum(gated * gated, axis=1, keepdims=True)
    square_ref[...] = jnp.broadcast_to(squares, (BLOCK, LANES)).T[0:8, :]


def gate_rows(gate, slots, y, query, carry, state, heads):
    rows, inner = y.shape
    fixed = lambda array: pl.BlockSpec(array.shape, lambda c: (0, 0))
    tiled = lambda array: pl.BlockSpec((BLOCK, array.shape[1]), lambda c: (c, 0))
    return pl.pallas_call(
        functools.partial(gate_kernel, heads),
        grid=(rows // BLOCK,),
        in_specs=[fixed(gate), fixed(slots), tiled(y), tiled(query), tiled(carry), fixed(state)],
        out_specs=[
            pl.BlockSpec((BLOCK, inner), lambda c: (c, 0)),
            pl.BlockSpec((8, BLOCK), lambda c: (0, c)),
        ],
        out_shape=[
            jax.ShapeDtypeStruct((rows, inner), F32),
            jax.ShapeDtypeStruct((8, rows), F32),
        ],
        cost_estimate=pl.CostEstimate(
            flops=5_000_000_000, bytes_accessed=16_000_000, transcendentals=rows * inner
        ),
    )(gate, slots, y, query, carry, state)


def body(
    xs, gate_in, bc_in, dt_in, placement, lengths,
    conv_x, conv_bc, a_log, dt_bias, d_skip, norm_gain, *, full_inner,
):
    shards = lax.axis_size("seq")
    mine = lax.axis_index("seq")
    rows, inner = xs.shape
    heads = a_log.shape[0]
    head_dim = inner // heads
    per = rows // shards
    width = conv_x.shape[0]
    place = jnp.broadcast_to(placement[None, :], (8, rows))
    local = placement % rows
    digits = jnp.stack([local // 32, local % 32], 1).astype(BF16)
    spare = jnp.zeros((rows, LANES - heads - 2), BF16)
    small = jnp.concatenate([bc_in, dt_in, digits, spare], 1)
    sent = send_rows(place, (xs, small), shards, RIM, width)
    arrived = lax.all_to_all(sent, "seq", split_axis=0, concat_axis=0, tiled=True)
    gate_sent = send_rows(place, (gate_in,), shards, 0, width)
    arrived, gate_sent = lax.optimization_barrier((arrived, gate_sent))
    gate = lax.all_to_all(gate_sent, "seq", split_axis=0, concat_axis=0, tiled=True)

    starts = jnp.concatenate(
        [jnp.cumsum(lengths) - lengths, jnp.asarray(mine * rows, jnp.int32)[None]]
    )
    taps = jnp.concatenate([conv_x, conv_bc], 1)
    head_rows = jnp.zeros((8, LANES), F32).at[0, :heads].set(a_log).at[1, :heads].set(dt_bias)
    skip = jnp.broadcast_to(jnp.repeat(d_skip, head_dim)[None, :], (8, inner))
    y, query, carry, slots, state = scan_blocks(
        starts, arrived.reshape(shards * (per + RIM), -1), taps, head_rows, skip, per, heads, rows
    )
    keep = jnp.repeat(carry[rows - 1, :heads], head_dim)[None, :]
    incoming = jnp.zeros_like(state)
    for hop in range(1, shards):
        onward = (keep * incoming + state).astype(BF16)
        came = lax.ppermute(onward, "seq", [(hop - 1, hop)])
        incoming = jnp.where(mine == hop, came.astype(F32), incoming)
    gate_slots = slots.reshape(8, shards, per + RIM)[:, :, :per].reshape(8, rows)
    gated, squares = gate_rows(
        gate.reshape(rows, inner), gate_slots, y, query, carry, incoming, heads
    )
    squares = lax.psum(squares[0], "head")
    result = gated * lax.rsqrt(squares / full_inner + 1e-05)[:, None] * norm_gain[None, :]
    return result.astype(BF16)


def solution(mesh):
    in_specs = (
        P(("parts", "seq"), "head"),
        P(("parts", "seq"), "head"),
        P(("parts", "seq"), None),
        P(("parts", "seq"), "head"),
        P(("parts", "seq")),
        P("parts"),
        P(None, "head"),
        P(),
        P("head"),
        P("head"),
        P("head"),
        P("head"),
    )
    out_specs = P(("parts", "seq"), "head")

    def whole(*args):
        step = functools.partial(body, full_inner=args[0].shape[1])
        return jax.shard_map(
            step, mesh=mesh, in_specs=in_specs, out_specs=out_specs, check_vma=False
        )(*args)

    return whole
```

time: 487 us -> 200 us (0.41); the launches traced: 478 us -> 199 us
  local copies, waits for them, and re-layouts: 236 us -> 10.3 us
  Pallas kernels: 0 us -> 55.3 us
  other arithmetic: 56.9 us -> 12.5 us
  blocking collectives: 51.7 us -> 7.81 us
  waiting for transfers between devices: 64.1 us -> 98.2 us
  matrix products: 23.7 us -> 0 us
  starting transfers between devices: 29.8 us -> 14.5 us
  between operations: 15 us -> 0.15 us
    dynamic_update_slice x8 -> x0, local copies, waits for them, and re-layouts: 136 us -> none  [body(): lax.scan(block_pass, empty, (split(conv_rows), split(key_rows), split(que...]
    pallas_call x0 -> x4, Pallas kernels: none -> 55.3 us  [the longest x1 29.7 us: scan_blocks(): pl.pallas_call(functools.partial(scan_kernel, per, heads), grid=(rows //...]
    unnamed x1 -> x0, blocking collectives: 46.1 us -> none
    gather x5 -> x0, local copies, waits for them, and re-layouts: 30.6 us -> none  [grouped(): return array[order].reshape((shards, per_dest) + array.shape[1:])]
    ppermute x1 -> x3, waiting for transfers between devices: 3.37 us -> 33.4 us  [body(): came = lax.ppermute(onward, 'seq', [(hop - 1, hop)])]
    dot_general x17 -> x0, matrix products: 23.7 us -> none  [the longest x4 12.7 us: block_pass(): outputs = jnp.einsum('tsh,shp->thp', mixing, inputs, precision=highest)]
    reshape x8 -> x1, local copies, waits for them, and re-layouts: 23.2 us -> 0.09 us  [body(): slots.reshape(8, shards, per + RIM)[:, :, :per].reshape(8, rows)]
    scatter x5 -> x2, local copies, waits for them, and re-layouts: 23.4 us -> 1.4 us  [body(): jnp.zeros((8, LANES), F32).at[0, :heads].set(a_log).at[1, :heads]]
  transfers between devices with their start and end apart: 7 -> 5, of which waited for: 4 -> 2; matrix products, arithmetic and copies ran while one was open for 56% -> 6% of each run, Pallas kernels for 0% -> 18%
where the time goes in v1:
time: 200 us; the launch traced here: 199 us
  waiting for transfers between devices  98.2 us (49%)
  Pallas kernels  55.3 us (28%)
  starting transfers between devices  14.5 us (7%)
  other arithmetic  12.5 us (6%)
  local copies, waits for them, and re-layouts  10.3 us (5%)
  blocking collectives  7.81 us (4%)
    all_to_all x1, waiting for transfers between devices, body(): lax.all_to_all(sent, 'seq', split_axis=0, concat_axis=0, tiled=True)  64.8 us
    ppermute x3, waiting for transfers between devices, body(): came = lax.ppermute(onward, 'seq', [(hop - 1, hop)])  33.4 us
    pallas_call x1, Pallas kernels, scan_blocks(): pl.pallas_call(functools.partial(scan_kernel, per, heads), grid=(rows //...  29.7 us
    pallas_call x2, Pallas kernels, send_rows(): pl.pallas_call(functools.partial(send_kernel, shards, per, rim, width), g...  14.5 us
    pallas_call x1, Pallas kernels, gate_rows(): pl.pallas_call(functools.partial(gate_kernel, heads), grid=(rows // BLOCK...  11.1 us
    psum x1, blocking collectives, body(): squares = lax.psum(squares[0], 'head')  7.81 us
    all_to_all x1, starting transfers between devices, body(): lax.all_to_all(gate_sent, 'seq', split_axis=0, concat_axis=0, tiled=True)  7.01 us
    all_to_all x1, starting transfers between devices, body(): lax.all_to_all(sent, 'seq', split_axis=0, concat_axis=0, tiled=True)  4.67 us
  transfers between devices with their start and end apart: 5, of which 2 were waited for; matrix products, arithmetic and copies ran while one was open for 6% of the time, Pallas kernels for 18%

profile of v1, /device:TPU:25, one launch (start us, length us, event | category | flops | bytes accessed | tf_op | source)
XLA Modules:
  0.0 198.7 jit_solution(4534134697958829037)
XLA Ops:
  0.0 0.7 fusion.2
  0.7 0.2 stack.13
  0.9 0.2 stack.12
  1.1 0.9 copy.15
  2.1 3.1 %concatenate.14.refs_1_ = bf16[1024,384]{1,0:T(8,128)(2,1)} concatenate(bf16[1024,256]{1,0:T(8,128)(2,1)} %param.18, bf16[1024,16]{1,0:T(8,128)(2,1)S(1)} %copy.15, bf16[1024,1]{1,0:T(8,128)(2,1)S(1)} %stack.12, bf16[1024,1]{1,0:T(8,128)(2,1)S(1)} %stack.13, bf16[1024,110]{1,0:T(8,128)(2,1)S(1)} %broadcast_in_dim.34), dimensions={1} | concatenate | bytes 1572864 | tf_op jit(solution)/shard_map/concatenate | solution.py:275
  5.2 1.3 broadcast_in_dim.33.place_ref
  6.5 8.0 %shard_map.118 = bf16[4,264,1664]{2,1,0:T(8,128)(2,1)} custom-call(s32[8,1024]{1,0:T(8,128)} %broadcast_in_dim.33.place_ref, bf16[1024,1280]{1,0:T(8,128)(2,1)} %refs_0_.2, bf16[1024,384]{1,0:T(8,128)(2,1)} %concatenate.14.refs_1_), custom_call_target="tpu_custom_call" | custom-call | flops 3489660928 | bytes 6815744 | tf_op jit(solution)/shard_map/pallas_call | solution.py:79
  14.5 4.7 %all-to-all-start = ((bf16[4,264,1664]{2,1,0:T(8,128)(2,1)}), bf16[4,264,1664]{2,1,0:T(8,128)(2,1)S(1)}, u32[]{:S(2)}, u32[]{:S(2)}) async-start(bf16[4,264,1664]{2,1,0:T(8,128)(2,1)} %shard_map.118), calls=%async_computation | async-start | bytes 7028736 | tf_op jit(solution)/shard_map/all_to_all | solution.py:277
  19.2 0.0 copy-done.6
  19.2 0.1 broadcast_in_dim.36
  19.2 0.1 broadcast_in_dim.37
  19.3 0.8 reduce-window.9
  20.2 0.7 scatter.6
  20.8 0.7 scatter.9.head_ref
  21.6 0.0 copy-start.5
  21.6 0.7 bitcast_subtract_fusion
  22.2 0.7 pad_add_fusion.start_ref
  22.9 0.0 copy-done.2
  22.9 0.0 copy-done.4
  22.9 0.6 pad_maximum_fusion.taps_ref
  23.5 6.5 %shard_map.119 = bf16[4,256,1280]{2,1,0:T(8,128)(2,1)} custom-call(s32[8,1024]{1,0:T(8,128)} %broadcast_in_dim.33.place_ref, bf16[1024,1280]{1,0:T(8,128)(2,1)} %refs_0_.3), custom_call_target="tpu_custom_call" | custom-call | flops 2684354560 | bytes 5242880 | tf_op jit(solution)/shard_map/pallas_call | solution.py:79
  30.0 0.0 copy-done.5
  30.0 64.8 %all-to-all-done = bf16[4,264,1664]{2,1,0:T(8,128)(2,1)S(1)} async-done(((bf16[4,264,1664]{2,1,0:T(8,128)(2,1)}), bf16[4,264,1664]{2,1,0:T(8,128)(2,1)S(1)}, u32[]{:S(2)}, u32[]{:S(2)}) %all-to-all-start) | async-done | bytes 3514400 | tf_op jit(solution)/shard_map/all_to_all | solution.py:277
  94.8 7.0 %all-to-all-start.1 = ((bf16[4,256,1280]{2,1,0:T(8,128)(2,1)}), bf16[4,256,1280]{2,1,0:T(8,128)(2,1)}, u32[]{:S(2)}, u32[]{:S(2)}) async-start(bf16[4,256,1280]{2,1,0:T(8,128)(2,1)} %shard_map.119), calls=%async_computation.1 | async-start | bytes 5242880 | tf_op jit(solution)/shard_map/all_to_all | solution.py:280
  101.8 0.6 broadcast_in_dim.38.skip_ref
  102.4 0.0 copy-done
  102.4 29.7 %shard_map.120 = (f32[1024,1280]{1,0:T(8,128)}, bf16[1024,128]{1,0:T(8,128)(2,1)}, f32[1024,128]{1,0:T(8,128)}, s32[8,1056]{1,0:T(8,128)}, f32[128,1280]{1,0:T(8,128)}) custom-call(s32[4]{0:T(128)} %pad_add_fusion.start_ref, bf16[1056,1664]{1,0:T(8,128)(2,1)} %bitcast.12, f32[4,1536]{1,0:T(4,128)} %pad_maximum_fusion.taps_ref, f32[8,128]{1,0:T(8,128)} %copy-done.5, ...), custom_call_target="tpu_custom_call" | custom-call | flops 20000000000 | bytes 12000000 | tf_op jit(solution)/shard_map/pallas_call | solution.py:192
  132.1 0.7 slice_bitcast_fusion
  132.8 0.1 broadcast_in_dim.39
  132.9 0.1 mul.45
  133.0 1.1 add_convert_fusion.2
  134.1 0.7 collective-permute-start
  134.8 0.0 collective-permute-done
  134.8 1.2 add_convert_fusion.1
  136.0 0.7 collective-permute-start.1
  136.7 0.0 collective-permute-done.1
  136.7 1.2 add_convert_fusion
  138.0 1.5 collective-permute-start.2
  139.5 0.1 reshape.108
  139.6 0.6 copy.19
  140.2 33.3 %collective-permute-done.2 = bf16[128,1280]{1,0:T(8,128)(2,1)S(1)} collective-permute-done((bf16[128,1280]{1,0:T(8,128)(2,1)S(1)}, bf16[128,1280]{1,0:T(8,128)(2,1)S(1)}, u32[]{:S(2)}, u32[]{:S(2)}) %collective-permute-start.2) | collective-permute-done | bytes 327712 | tf_op jit(solution)/shard_map/ppermute | solution.py:295
  173.5 1.0 convert_select_fusion.state_ref
  174.5 0.0 all-to-all-done.1
  174.5 11.1 %shard_map.121 = (f32[1024,1280]{1,0:T(8,128)}, f32[8,1024]{1,0:T(8,128)}) custom-call(bf16[1024,1280]{1,0:T(8,128)(2,1)} %bitcast.gate_ref, s32[8,1024]{1,0:T(8,128)} %bitcast.13, f32[1024,1280]{1,0:T(8,128)} %get-tuple-element.41.y_ref, bf16[1024,128]{1,0:T(8,128)(2,1)} %get-tuple-element.42.query_ref, f32[1024,128]{1,0:T(8,128)} %get-tuple-element.43.carry_ref, ...), custom_call_target="tpu_custom_call" | custom-call | flops 5000000000 | bytes 16000000 | tf_op jit(solution)/shard_map/pallas_call | solution.py:242
  185.6 0.8 slice.46
  186.4 7.8 %psum.7 = f32[1024]{0:T(1024)S(1)} all-reduce(f32[1024]{0:T(1024)S(1)} %bitcast.14), channel_id=1, replica_groups=mesh['parts'=2,'seq'=4,'head'=4] {'head'}, use_global_device_ids=true, to_apply=%region_1.2 | all-reduce | flops 1024 | bytes 8192 | tf_op jit(solution)/shard_map/psum | solution.py:301
  194.2 0.0 copy-done.3
  194.2 4.5 %multiply_convert_fusion = bf16[1024,1280]{1,0:T(8,128)(2,1)} fusion(f32[1024,1280]{1,0:T(8,128)} %get-tuple-element.45, f32[1280]{0:T(1024)S(1)} %copy-done.3, f32[1024]{0:T(1024)S(1)} %add_rsqrt_fusion), kind=kLoop, calls=%fused_computation | loop fusion | flops 3932160 | bytes 7873536 | tf_op jit(solution)/shard_map/convert_element_type | solution.py:303
  (11 shorter events, 0.1 us)
Async XLA Ops:
  14.5 4.7 %copy-start.6 = (f32[16]{0:T(128)S(1)}, f32[16]{0:T(128)}, u32[]{:S(2)}) copy-start(f32[16]{0:T(128)} %param.26) | copy-start | bytes 196
  14.5 8.4 %copy-start.2 = (f32[4,1280]{1,0:T(4,128)S(1)}, f32[4,1280]{1,0:T(4,128)}, u32[]{:S(2)}) copy-start(f32[4,1280]{1,0:T(4,128)} %param.22) | copy-start | bytes 61444
  14.5 8.4 %copy-start.4 = (f32[4,256]{1,0:T(4,128)S(1)}, f32[4,256]{1,0:T(4,128)}, u32[]{:S(2)}) copy-start(f32[4,256]{1,0:T(4,128)} %param.23) | copy-start | bytes 12292
  14.5 80.3 %all-to-all-start = ((bf16[4,264,1664]{2,1,0:T(8,128)(2,1)}), bf16[4,264,1664]{2,1,0:T(8,128)(2,1)S(1)}, u32[]{:S(2)}, u32[]{:S(2)}) async-start(bf16[4,264,1664]{2,1,0:T(8,128)(2,1)} %shard_map.118), calls=%async_computation | async-start | bytes 7028736 | tf_op jit(solution)/shard_map/all_to_all | solution.py:277
  21.6 8.4 %copy-start.5 = (f32[8,128]{1,0:T(8,128)}, f32[8,128]{1,0:T(8,128)S(1)}, u32[]{:S(2)}) copy-start(f32[8,128]{1,0:T(8,128)S(1)} %scatter.9.head_ref) | copy-start | bytes 12292
  94.8 7.6 %copy-start = (bf16[4,264,1664]{2,1,0:T(8,128)(2,1)}, bf16[4,264,1664]{2,1,0:T(8,128)(2,1)S(1)}, u32[]{:S(2)}) copy-start(bf16[4,264,1664]{2,1,0:T(8,128)(2,1)S(1)} %all-to-all-done) | copy-start | bytes 10543108
  94.8 79.7 %all-to-all-start.1 = ((bf16[4,256,1280]{2,1,0:T(8,128)(2,1)}), bf16[4,256,1280]{2,1,0:T(8,128)(2,1)}, u32[]{:S(2)}, u32[]{:S(2)}) async-start(bf16[4,256,1280]{2,1,0:T(8,128)(2,1)} %shard_map.119), calls=%async_computation.1 | async-start | bytes 5242880 | tf_op jit(solution)/shard_map/all_to_all | solution.py:280
  132.1 7.3 %copy-start.1 = (s32[8,1056]{1,0:T(8,128)S(1)}, s32[8,1056]{1,0:T(8,128)}, u32[]{:S(2)}) copy-start(s32[8,1056]{1,0:T(8,128)} %get-tuple-element.40) | copy-start | bytes 101380
  134.1 0.7 collective-permute-start
  136.0 0.7 collective-permute-start.1
  138.0 35.6 %collective-permute-start.2 = (bf16[128,1280]{1,0:T(8,128)(2,1)S(1)}, bf16[128,1280]{1,0:T(8,128)(2,1)S(1)}, u32[]{:S(2)}, u32[]{:S(2)}) collective-permute-start(bf16[128,1280]{1,0:T(8,128)(2,1)S(1)} %add_convert_fusion), channel_id=1, source_target_pairs={{8,12},{9,13},{10,14},{11,15},{24,28},{25,29},{26,30},{27,31}} | collective-permute-start | bytes 983048 | tf_op jit(solution)/shard_map/ppermute | solution.py:295
  174.5 19.7 %copy-start.3 = (f32[1280]{0:T(1024)S(1)}, f32[1280]{0:T(1024)}, u32[]{:S(2)}) copy-start(f32[1280]{0:T(1024)} %param.27) | copy-start | bytes 15364

commit v2 on v1

v2 whole, which is shorter than its diff:
```python
import functools

import jax
import jax.numpy as jnp
from jax import lax
from jax.experimental import pallas as pl
from jax.experimental.pallas import tpu as pltpu
from jax.sharding import PartitionSpec as P

BLOCK = 256
LANES = 128
RIM = 8
HIGHEST = lax.Precision.HIGHEST
MESH = pl.DeviceIdType.MESH
F32 = jnp.float32
BF16 = jnp.bfloat16


def iota(shape, dim):
    return lax.broadcasted_iota(jnp.int32, shape, dim)


def dot(a, b, dims=((1,), (0,))):
    return lax.dot_general(a, b, (dims, ((), ())), preferred_element_type=F32)


def halves(value):
    high = value.astype(BF16)
    return high, (value - high.astype(F32)).astype(BF16)


def dot_left(a, b):
    high, low = halves(a)
    return dot(high, b) + dot(low, b)


def dot_right(a, b):
    high, low = halves(b)
    return dot(jnp.concatenate([a, a], 1), jnp.concatenate([high, low], 0))


def dot_turned(a, b):
    high, low = halves(b)
    dims = ((0,), (0,))
    return dot(a, high, dims) + dot(a, low, dims)


def expanded(value, heads, head_dim, width):
    head, channel = iota((LANES, width), 0), iota((LANES, width), 1)
    head = jnp.where(head < heads, head, head - LANES // 2)
    inside = (channel >= head * head_dim) & (channel < (head + 1) * head_dim)
    high, low = halves(value)
    low = pltpu.roll(low.astype(F32), LANES // 2, 1)
    lane = iota((1, LANES), 1)
    both = jnp.where(lane < LANES // 2, high.astype(F32), low)
    return dot(both.astype(BF16), inside.astype(F32).astype(BF16))


def picked(place, slot, dest, per, rim, width):
    rows = place.shape[1]
    target = lax.shift_right_logical(place, rows.bit_length() - 1)
    offset = place - dest * rows
    key = jnp.where(target == dest, slot, -1)
    if rim:
        key = jnp.where((offset < 0) & (offset >= 1 - width), offset + (width - 1 + per), key)
    return (iota((per + rim, rows), 0) == key).astype(F32).astype(BF16)


def greet(axes):
    barrier = pltpu.get_barrier_semaphore()
    for axis in axes:
        count, me = lax.axis_size(axis), lax.axis_index(axis)

        def signal(i, _, axis=axis, count=count, me=me):
            pl.semaphore_signal(
                barrier, inc=1, device_id={axis: lax.rem(me + i, count)}, device_id_type=MESH
            )
            return 0

        lax.fori_loop(1, count, signal, 0)
    pl.semaphore_wait(barrier, sum(lax.axis_size(axis) - 1 for axis in axes))


def remote(source, target, sends, receives, axis, offset):
    count, me = lax.axis_size(axis), lax.axis_index(axis)
    return pltpu.make_async_remote_copy(
        src_ref=source,
        dst_ref=target,
        send_sem=sends,
        recv_sem=receives,
        device_id={axis: lax.rem(me + offset, count)},
        device_id_type=MESH,
    )


def move_kernel(
    width, heads, place_ref, x_ref, small_ref, gate_ref, arrived_ref, tails_ref, gate_out_ref,
    x_send, small_send, x_sems, small_sems, tail_sems,
):
    shards, peers = lax.axis_size("seq"), lax.axis_size("head")
    me, own = lax.axis_index("seq"), lax.axis_index("head")
    rows = place_ref.shape[1]
    per = rows // shards
    greet(("seq", "head"))
    place = place_ref[0:1, :]
    groups = -(-shards // 16) * 16
    target = lax.shift_right_logical(place, rows.bit_length() - 1)
    chosen = iota((groups, rows), 0) == target
    before = (iota((rows, rows), 0) < iota((rows, rows), 1)).astype(F32).astype(BF16)
    counts = dot(chosen.astype(F32).astype(BF16), before)
    slot = jnp.sum(jnp.where(chosen, counts, 0.0), axis=0, keepdims=True).astype(jnp.int32)
    local = place & (rows - 1)
    line = iota((LANES, rows), 0)
    digits = jnp.where(line == heads, local >> 5, jnp.where(line == heads + 1, local & 31, 0))
    digits = digits.astype(F32).astype(BF16)

    def x_copy(i):
        return remote(
            x_send.at[i], arrived_ref.at[me], x_sems.at[0, i], x_sems.at[1, i], "seq", i
        )

    def small_copy(i):
        return remote(
            small_send.at[i], tails_ref.at[own, me], small_sems.at[0, i], small_sems.at[1, i], "seq", i
        )

    def tail_copy(i):
        return remote(
            tails_ref.at[own], tails_ref.at[own], tail_sems.at[0, i], tail_sems.at[1, i], "head", i
        )

    def small_step(i, _):
        pick = picked(place, slot, lax.rem(me + i, shards), per, RIM, width)
        values = dot(pick, small_ref[...]) + dot(pick, digits, ((1,), (1,)))
        small_send[i] = values.astype(BF16)
        return 0

    def x_step(i, _):
        pick = picked(place, slot, lax.rem(me + i, shards), per, RIM, width)
        x_send[i] = dot(pick, x_ref[...]).astype(BF16)

        @pl.when(i > 1)
        def _():
            x_copy(i - 1).start()

        return 0

    def each(first, last, action):
        def step(i, _):
            action(i)
            return 0

        lax.fori_loop(first, last, step, 0)

    lax.fori_loop(0, shards, small_step, 0)
    lax.fori_loop(1, 2, x_step, 0)
    each(1, shards, lambda i: small_copy(i).start())
    lax.fori_loop(2, shards, x_step, 0)
    tails_ref[own, me] = small_send[0]
    pick = picked(place, slot, me, per, RIM, width)
    arrived_ref[me] = dot(pick, x_ref[...]).astype(BF16)
    x_copy(shards - 1).start()

    def gate_step(dest, _):
        pick = picked(place, slot, dest, per, 0, width)
        gate_out_ref[dest] = dot(pick, gate_ref[...]).astype(BF16)
        return 0

    lax.fori_loop(0, shards, gate_step, 0)
    each(1, shards, lambda i: small_copy(i).wait())
    each(1, peers, lambda i: tail_copy(i).start())
    each(1, peers, lambda i: tail_copy(i).wait())
    each(1, shards, lambda i: x_copy(i).wait())


def move_rows(place, xs, small, gate, width, heads):
    shards, peers = lax.axis_size("seq"), lax.axis_size("head")
    rows, inner = xs.shape
    per = rows // shards
    vmem = pl.BlockSpec(memory_space=pltpu.VMEM)
    return pl.pallas_call(
        functools.partial(move_kernel, width, heads),
        in_specs=[vmem] * 4,
        out_specs=[vmem] * 3,
        out_shape=[
            jax.ShapeDtypeStruct((shards, per + RIM, inner), BF16),
            jax.ShapeDtypeStruct((peers, shards, per + RIM, LANES), BF16),
            jax.ShapeDtypeStruct((shards, per, inner), BF16),
        ],
        scratch_shapes=[
            pltpu.VMEM((shards, per + RIM, inner), BF16),
            pltpu.VMEM((shards, per + RIM, LANES), BF16),
            pltpu.SemaphoreType.DMA((2, shards)),
            pltpu.SemaphoreType.DMA((2, shards)),
            pltpu.SemaphoreType.DMA((2, peers)),
        ],
        compiler_params=pltpu.CompilerParams(
            collective_id=0, has_side_effects=True, vmem_limit_bytes=56 << 20
        ),
    )(place, xs, small, gate)


def doc_at(start_ref, position):
    total = jnp.where(start_ref[0] <= position, 1, 0)
    for j in range(1, start_ref.shape[0] - 1):
        total = total + jnp.where(start_ref[j] <= position, 1, 0)
    return total


def scan_step(
    chunk, chunks, per, heads, start_ref, arrived_ref, bc_ref, tail_ref, taps_ref, head_ref,
    skip_ref, y_ref, query_ref, carry_ref, slot_ref, state_ref, total_ref,
):
    width = taps_ref.shape[0]
    inner = y_ref.shape[1]
    head_dim = inner // heads
    rows_in = arrived_ref.shape[0]
    base = start_ref[start_ref.shape[0] - 1]
    origin = base + chunk * BLOCK
    here = pl.ds(pl.multiple_of(chunk * BLOCK, BLOCK), BLOCK)

    wanted = iota((BLOCK + RIM, rows_in), 0) + (chunk * BLOCK - RIM)
    pick = (wanted == slot_ref[0:1, :]).astype(F32).astype(BF16)
    column = iota((BLOCK, 1), 0) + origin
    docs = doc_at(start_ref, column)
    matches = [None] + [
        (doc_at(start_ref, column - lag) == docs) & (column >= lag) for lag in range(1, width)
    ]

    def convolved(packed, first):
        count = packed.shape[1]
        total = taps_ref[0:1, first : first + count] * packed[RIM:, :]
        for lag in range(1, width):
            part = taps_ref[lag : lag + 1, first : first + count] * packed[RIM - lag : RIM - lag + BLOCK, :]
            total = total + jnp.where(matches[lag], part, 0.0)
        return (total * jax.nn.sigmoid(total)).astype(BF16)

    x = convolved(dot(pick, arrived_ref[...]), 0)
    both = convolved(dot(pick, bc_ref[...]), inner)
    keys, query = both[:, :LANES], both[:, LANES:]
    query_ref[here, :] = query
    raw = dot(pick, tail_ref[...])[RIM:, :]
    raw = raw + head_ref[1:2, :]
    lane = iota((1, LANES), 1)
    step = jnp.maximum(raw, 0.0) + jnp.log1p(jnp.exp(-jnp.abs(raw)))
    step = jnp.where(lane < heads, step, 0.0)
    rate = jnp.exp(head_ref[0:1, :])
    decay = -rate * step
    lower = iota((BLOCK, BLOCK), 0) >= iota((BLOCK, BLOCK), 1)
    sums = jnp.dot(lower.astype(F32), decay, precision=HIGHEST, preferred_element_type=F32)
    sums_t = sums.T
    step_t = step.T
    docs_row = doc_at(start_ref, iota((1, BLOCK), 1) + origin)
    linked = lower & (docs == docs_row)
    scores = jnp.where(linked, dot(query, keys, ((1,), (1,))), 0.0)
    doc_before = doc_at(start_ref, origin - 1)
    doc_before = jnp.where(origin > 0, doc_before, 0)
    doc_base = jnp.where(base > 0, doc_at(start_ref, base - 1), 0)
    doc_last = doc_at(start_ref, origin + BLOCK - 1)
    carried = jnp.where(docs == doc_before, jnp.exp(sums), 0.0)
    last = sums[BLOCK - 1 : BLOCK, :]
    closing = jnp.where(docs == doc_last, jnp.exp(jnp.minimum(last - sums, 0.0)), 0.0) * step
    before = total_ref[0:1, :]
    carry_ref[here, :] = jnp.where(docs == doc_base, jnp.exp(before + sums), 0.0)
    total_ref[...] = jnp.broadcast_to(before + last, total_ref.shape)

    carried_all = expanded(carried, heads, head_dim, inner)
    state = state_ref[...]
    x32 = x.astype(F32)
    y_ref[here, :] = carried_all * dot_right(query, state) + skip_ref[0:1, :] * x32
    weighted = expanded(closing, heads, head_dim, inner) * x32
    state_ref[...] = carried_all[BLOCK - 1 : BLOCK, :] * state + dot_turned(keys, weighted)

    for head in range(heads):
        first, end = head * head_dim, (head + 1) * head_dim
        low, high = first // LANES * LANES, -(-end // LANES) * LANES
        gap = sums[:, head : head + 1] - sums_t[head : head + 1, :]
        weight = jnp.exp(jnp.minimum(gap, 0.0)) * step_t[head : head + 1, :] * scores
        channel = iota((1, high - low), 1) + low
        own = jnp.where((channel >= first) & (channel < end), x32[:, low:high], 0.0).astype(BF16)
        y_ref[here, low:high] += dot_left(weight, own)


def start_step(per, heads, tail_ref, slot_ref, gate_slot_ref):
    shards = lax.axis_size("seq")
    block = per + RIM
    lane, row = iota((16, LANES), 1), iota((16, LANES), 0)
    factor = jnp.where(lane == heads, 32.0, jnp.where(lane == heads + 1, 1.0, 0.0))
    factor = jnp.where(row == 0, factor, 0.0).astype(BF16)
    place = dot(factor, tail_ref[...], ((1,), (1,)))[0:8, :].astype(jnp.int32)
    within = iota((8, shards * block), 1) % block
    slot_ref[...] = jnp.where(within >= per, place - per * shards, place)
    for source in range(shards):
        gate_slot_ref[:, source * per : (source + 1) * per] = place[
            :, source * block : source * block + per
        ]


def layer_kernel(
    per, heads, full_inner, start_ref, arrived_ref, bc_ref, tail_ref, taps_ref, head_ref, skip_ref,
    gain_ref, gate_ref, out_ref,
    y_ref, query_ref, carry_ref, slot_ref, gate_slot_ref, state_ref, total_ref,
    gate_in, came, onward, incoming, squares, gate_sems, own_sem, state_sems, square_sems,
):
    shards, peers = lax.axis_size("seq"), lax.axis_size("head")
    me, own = lax.axis_index("seq"), lax.axis_index("head")
    step = pl.program_id(0)
    rows, inner = y_ref.shape
    chunks = rows // BLOCK
    head_dim = inner // heads
    pieces, _, wide = came.shape

    def gate_copy(i):
        to = lax.rem(me + i, shards)
        return remote(
            gate_ref.at[to], gate_in.at[me], gate_sems.at[0, i], gate_sems.at[1, i], "seq", i
        )

    def own_copy():
        return pltpu.make_async_copy(gate_ref.at[me], gate_in.at[me], own_sem)

    def state_copy(piece):
        return remote(
            onward.at[piece], came.at[piece], state_sems.at[0, piece], state_sems.at[1, piece], "seq", 1
        )

    def square_copy(chunk, i):
        return remote(
            squares.at[own, chunk], squares.at[own, chunk],
            square_sems.at[0, chunk, i], square_sems.at[1, chunk, i], "head", i,
        )

    def each(first, last, action):
        def once(i, _):
            action(i)
            return 0

        lax.fori_loop(first, last, once, 0)

    @pl.when(step == 0)
    def _():
        greet(("seq", "head"))
        each(1, shards, lambda i: gate_copy(i).start())
        own_copy().start()
        start_step(per, heads, tail_ref, slot_ref, gate_slot_ref)
        state_ref[...] = jnp.zeros_like(state_ref)
        total_ref[...] = jnp.zeros_like(total_ref)

    @pl.when(step < chunks)
    def _():
        scan_step(
            step, chunks, per, heads, start_ref, arrived_ref, bc_ref, tail_ref, taps_ref, head_ref,
            skip_ref, y_ref, query_ref, carry_ref, slot_ref, state_ref, total_ref,
        )

    @pl.when(step == chunks - 1)
    def _():
        tail_rows = carry_ref[rows - 8 : rows, :]
        keep = expanded(tail_rows, heads, head_dim, inner)[7:8, :]
        for piece in range(pieces):
            span = slice(piece * wide, (piece + 1) * wide)

            @pl.when(me > 0)
            def _():
                state_copy(piece).wait_recv()
                incoming[:, span] = came[piece].astype(F32)

            @pl.when(me == 0)
            def _():
                incoming[:, span] = jnp.zeros((LANES, wide), F32)

            passed = keep[:, span] * incoming[:, span] + state_ref[:, span]
            onward[piece] = passed.astype(BF16)
            if piece > 0:

                @pl.when(me < shards - 1)
                def _():
                    state_copy(piece - 1).start()

        state_ref[...] = incoming[...]

        @pl.when(me < shards - 1)
        def _():
            state_copy(pieces - 1).start()
            for piece in range(pieces):
                state_copy(piece).wait_send()

        each(1, shards, lambda i: gate_copy(i).wait())
        own_copy().wait()

    @pl.when((step > chunks) & (step <= 2 * chunks))
    def _():
        each(1, peers, lambda i: square_copy(step - chunks - 1, i).start())

    @pl.when((step >= chunks) & (step < 2 * chunks))
    def _():
        chunk = step - chunks
        here = pl.ds(pl.multiple_of(chunk * BLOCK, BLOCK), BLOCK)
        wanted = iota((BLOCK, rows), 0) + chunk * BLOCK
        pick = (wanted == gate_slot_ref[0:1, :]).astype(F32).astype(BF16)
        gate = dot(pick, gate_in[...].reshape(rows, inner))
        carried = expanded(carry_ref[here, :], heads, head_dim, inner)
        y = y_ref[here, :] + carried * dot(query_ref[here, :], state_ref[...].astype(BF16))
        gated = y * (gate * jax.nn.sigmoid(gate))
        y_ref[here, :] = gated
        total = jnp.sum(gated * gated, axis=1, keepdims=True)
        squares[own, chunk] = jnp.broadcast_to(total, (BLOCK, LANES)).T[0:8, :]

    @pl.when(step >= 2 * chunks)
    def _():
        chunk = step - 2 * chunks
        here = pl.ds(pl.multiple_of(chunk * BLOCK, BLOCK), BLOCK)
        each(1, peers, lambda i: square_copy(chunk, i).wait())
        total = squares[0, chunk]
        for peer in range(1, peers):
            total = total + squares[peer, chunk]
        scale = lax.rsqrt(total / full_inner + 1e-05)
        scale = jnp.concatenate([scale] * (LANES // 8), 0).T[:, 0:1]
        out_ref[...] = (y_ref[here, :] * scale * gain_ref[0:1, :]).astype(BF16)


def layer(starts, arrived, bc, tail, taps, head_rows, skip, gain, gate, per, heads, rows, full_inner):
    shards, peers = lax.axis_size("seq"), lax.axis_size("head")
    rows_in, inner = arrived.shape
    chunks = rows // BLOCK
    wide = 2 * LANES
    vmem = pl.BlockSpec(memory_space=pltpu.VMEM)
    return pl.pallas_call(
        functools.partial(layer_kernel, per, heads, full_inner),
        grid=(3 * chunks,),
        in_specs=[pl.BlockSpec(memory_space=pltpu.SMEM)]
        + [vmem] * 7
        + [pl.BlockSpec(memory_space=pl.ANY)],
        out_specs=pl.BlockSpec((BLOCK, inner), lambda k: (jnp.maximum(k - 2 * chunks, 0), 0)),
        out_shape=jax.ShapeDtypeStruct((rows, inner), BF16),
        scratch_shapes=[
            pltpu.VMEM((rows, inner), F32),
            pltpu.VMEM((rows, LANES), BF16),
            pltpu.VMEM((rows, LANES), F32),
            pltpu.VMEM((8, rows_in), jnp.int32),
            pltpu.VMEM((8, rows), jnp.int32),
            pltpu.VMEM((LANES, inner), F32),
            pltpu.VMEM((8, LANES), F32),
            pltpu.VMEM((shards, per, inner), BF16),
            pltpu.VMEM((inner // wide, LANES, wide), BF16),
            pltpu.VMEM((inner // wide, LANES, wide), BF16),
            pltpu.VMEM((LANES, inner), F32),
            pltpu.VMEM((peers, chunks, 8, BLOCK), F32),
            pltpu.SemaphoreType.DMA((2, shards)),
            pltpu.SemaphoreType.DMA,
            pltpu.SemaphoreType.DMA((2, inner // wide)),
            pltpu.SemaphoreType.DMA((2, chunks, peers)),
        ],
        compiler_params=pltpu.CompilerParams(
            collective_id=1, has_side_effects=True, vmem_limit_bytes=60 << 20
        ),
    )(starts, arrived, bc, tail, taps, head_rows, skip, gain, gate)


def body(
    xs, gate_in, bc_in, dt_in, placement, lengths,
    conv_x, conv_bc, a_log, dt_bias, d_skip, norm_gain, *, full_inner,
):
    shards = lax.axis_size("seq")
    mine = lax.axis_index("seq")
    rows, inner = xs.shape
    heads = a_log.shape[0]
    head_dim = inner // heads
    per = rows // shards
    width = conv_x.shape[0]
    place = placement[None, :]
    quarter = bc_in.shape[1] // lax.axis_size("head")
    bc_own = lax.dynamic_slice_in_dim(bc_in, lax.axis_index("head") * quarter, quarter, 1)
    spare = jnp.zeros((rows, LANES - heads - quarter), BF16)
    small = jnp.concatenate([dt_in, spare, bc_own], 1)

    arrived, tails, gate = move_rows(place, xs, small, gate_in, width, heads)
    tails = tails.reshape(tails.shape[0], -1, LANES)
    bc = tails[:, :, LANES - quarter :].transpose(1, 0, 2).reshape(tails.shape[1], -1)
    starts = jnp.concatenate(
        [jnp.cumsum(lengths) - lengths, jnp.asarray(mine * rows, jnp.int32)[None]]
    )
    taps = jnp.concatenate([conv_x, conv_bc], 1)
    head_rows = jnp.zeros((8, LANES), F32).at[0, :heads].set(a_log).at[1, :heads].set(dt_bias)
    skip = jnp.broadcast_to(jnp.repeat(d_skip, head_dim)[None, :], (8, inner))
    gain = jnp.broadcast_to(norm_gain[None, :], (8, inner))
    tail = lax.dynamic_index_in_dim(tails, lax.axis_index("head"), 0, keepdims=False)
    return layer(
        starts, arrived.reshape(shards * (per + RIM), inner), bc, tail, taps, head_rows, skip,
        gain, gate, per, heads, rows, full_inner,
    )


def solution(mesh):
    in_specs = (
        P(("parts", "seq"), "head"),
        P(("parts", "seq"), "head"),
        P(("parts", "seq"), None),
        P(("parts", "seq"), "head"),
        P(("parts", "seq")),
        P("parts"),
        P(None, "head"),
        P(),
        P("head"),
        P("head"),
        P("head"),
        P("head"),
    )
    out_specs = P(("parts", "seq"), "head")

    def whole(*args):
        step = functools.partial(body, full_inner=args[0].shape[1])
        return jax.shard_map(
            step, mesh=mesh, in_specs=in_specs, out_specs=out_specs, check_vma=False
        )(*args)

    return whole
```

time: 200 us -> 178 us (0.89)
  Pallas kernels: 55.3 us -> 159 us
  waiting for transfers between devices: 98.2 us -> 0 us
  starting transfers between devices: 14.5 us -> 0 us
  other arithmetic: 12.5 us -> 4.34 us
  blocking collectives: 7.81 us -> 0 us
  local copies, waits for them, and re-layouts: 10.3 us -> 13.6 us
    pallas_call x4 -> x2, Pallas kernels: 55.3 us -> 159 us  [the longest x1 84.7 us: layer(): pl.pallas_call(functools.partial(layer_kernel, per, heads, full_inner), g...]
    all_to_all x2 -> x0, waiting for transfers between devices: 64.8 us -> none  [the longest x1 64.8 us: body(): lax.all_to_all(sent, 'seq', split_axis=0, concat_axis=0, tiled=True)]
    ppermute x3 -> x0, waiting for transfers between devices: 33.4 us -> none  [body(): came = lax.ppermute(onward, 'seq', [(hop - 1, hop)])]
    all_to_all x2 -> x0, starting transfers between devices: 11.7 us -> none  [the longest x1 7.01 us: body(): lax.all_to_all(gate_sent, 'seq', split_axis=0, concat_axis=0, tiled=True)]
    convert_element_type x4 -> x0, other arithmetic: 8.06 us -> none  [the longest x1 4.48 us: body(): return result.astype(BF16)]
    psum x1 -> x0, blocking collectives: 7.81 us -> none  [body(): squares = lax.psum(squares[0], 'head')]
    unnamed x16 -> x7, local copies, waits for them, and re-layouts: 1.56 us -> 4.94 us
    concatenate x1, local copies, waits for them, and re-layouts: 3.09 us -> 0.08 us  [body(): small = jnp.concatenate([dt_in, spare, bc_own], 1)]
  transfers between devices with their start and end apart: 5 -> 0, of which waited for: 2 -> 0; matrix products, arithmetic and copies ran while one was open for 6% -> 0% of each run, Pallas kernels for 18% -> 0%
where the time goes in v2:
time: 178 us; the launch traced here: 177 us
  Pallas kernels  159 us (89%)
  local copies, waits for them, and re-layouts  13.6 us (8%)
  other arithmetic  4.34 us (2%)
    pallas_call x1, Pallas kernels, layer(): pl.pallas_call(functools.partial(layer_kernel, per, heads, full_inner), g...  84.7 us
    pallas_call x1, Pallas kernels, move_rows(): pl.pallas_call(functools.partial(move_kernel, width, heads), in_specs=[vm...  74.7 us
    unnamed x7, local copies, waits for them, and re-layouts  4.94 us

profile of v2, /device:TPU:25, one launch (start us, length us, event | category | flops | bytes accessed | tf_op | source)
XLA Modules:
  0.0 177.4 jit_solution(9678562982014878089)
XLA Ops:
  0.0 0.0 copy-start
  0.0 0.9 reduce-window.9
  0.9 0.7 bitcast_subtract_fusion
  1.5 0.6 pad_add_fusion.start_ref
  2.1 0.1 pad.11.clone
  2.2 0.7 scatter.6
  2.8 0.7 scatter.9.head_ref
  3.6 0.0 copy-start.1
  3.6 0.7 broadcast_in_dim.29
  4.3 0.1 broadcast_in_dim.30
  4.4 1.4 pad_maximum_fusion.1.taps_ref
  5.8 0.6 broadcast_in_dim.31.skip_ref
  6.4 1.3 broadcast_in_dim.32.gain_ref
  7.7 0.0 copy-done
  7.7 0.1 constant_dynamic-slice_fusion
  7.9 0.9 copy.15
  8.8 0.9 pad_maximum_fusion.small_ref
  9.7 74.7 %shard_map.118 = (bf16[4,264,1280]{2,1,0:T(8,128)(2,1)}, bf16[4,4,264,128]{3,2,1,0:T(8,128)(2,1)}, bf16[4,256,1280]{2,1,0:T(8,128)(2,1)}) custom-call(s32[1,1024]{1,0:T(1,128)} %bitcast.18, bf16[1024,1280]{1,0:T(8,128)(2,1)} %x_ref.1, bf16[1024,128]{1,0:T(8,128)(2,1)} %pad_maximum_fusion.small_ref, bf16[1024,1280]{1,0:T(8,128)(2,1)} %gate_ref.1), custom_call_target="tpu_custom_call" | custom-call | tf_op jit(solution)/shard_map/pallas_call | solution.py:181
  84.4 0.0 copy-done.1
  84.4 1.7 dynamic-slice_bitcast_fusion.tail_ref
  86.1 1.6 slice.39
  87.7 0.6 copy.18
  88.3 1.0 copy.17.bc_ref
  89.3 84.7 %shard_map.119 = bf16[1024,1280]{1,0:T(8,128)(2,1)} custom-call(s32[4]{0:T(128)} %pad_add_fusion.start_ref, bf16[1056,1280]{1,0:T(8,128)(2,1)} %bitcast.14, bf16[1056,256]{1,0:T(8,128)(2,1)} %copy.17.bc_ref, bf16[1056,128]{1,0:T(8,128)(2,1)} %dynamic-slice_bitcast_fusion.tail_ref, f32[4,1536]{1,0:T(4,128)} %pad_maximum_fusion.1.taps_ref, ...), custom_call_target="tpu_custom_call" | custom-call | tf_op jit(solution)/shard_map/pallas_call | solution.py:428
  174.0 3.4 %copy.21 = bf16[1024,1280]{1,0:T(8,128)(2,1)} copy(bf16[1024,1280]{1,0:T(8,128)(2,1)} %shard_map.119) | data formatting | bytes 5242880
  (1 shorter events, 0.0 us)
Async XLA Ops:
  0.0 7.7 %copy-start = (bf16[1024,256]{1,0:T(8,128)(2,1)S(1)}, bf16[1024,256]{1,0:T(8,128)(2,1)}, u32[]{:S(2)}) copy-start(bf16[1024,256]{1,0:T(8,128)(2,1)} %param.18) | copy-start | bytes 1572868
  3.6 80.8 %copy-start.1 = (f32[8,128]{1,0:T(8,128)}, f32[8,128]{1,0:T(8,128)S(1)}, u32[]{:S(2)}) copy-start(f32[8,128]{1,0:T(8,128)S(1)} %scatter.9.head_ref) | copy-start | bytes 12292

commit v3 on v2

--- a/solution.py
+++ b/solution.py
@@ -93,9 +93,17 @@
     )
 
 
-def move_kernel(
-    width, heads, place_ref, x_ref, small_ref, gate_ref, arrived_ref, tails_ref, gate_out_ref,
-    x_send, small_send, x_sems, small_sems, tail_sems,
+def each(first, last, action):
+    def once(i, _):
+        action(i)
+        return 0
+
+    lax.fori_loop(first, last, once, 0)
+
+
+def move_step(
+    width, heads, place_ref, x_ref, small_ref, gate_ref, arrived_ref, tails_ref, gate_in,
+    x_send, small_send, gate_send, x_sems, small_sems, tail_sems, gate_copy,
 ):
     shards, peers = lax.axis_size("seq"), lax.axis_size("head")
     me, own = lax.axis_index("seq"), lax.axis_index("head")
@@ -145,13 +153,6 @@
 
         return 0
 
-    def each(first, last, action):
-        def step(i, _):
-            action(i)
-            return 0
-
-        lax.fori_loop(first, last, step, 0)
-
     lax.fori_loop(0, shards, small_step, 0)
     lax.fori_loop(1, 2, x_step, 0)
     each(1, shards, lambda i: small_copy(i).start())
@@ -161,102 +162,96 @@
     arrived_ref[me] = dot(pick, x_ref[...]).astype(BF16)
     x_copy(shards - 1).start()
 
-    def gate_step(dest, _):
-        pick = picked(place, slot, dest, per, 0, width)
-        gate_out_ref[dest] = dot(pick, gate_ref[...]).astype(BF16)
+    def gate_step(i, _):
+        pick = picked(place, slot, lax.rem(me + i, shards), per, 0, width)
+        gate_send[i] = dot(pick, gate_ref[...]).astype(BF16)
+
+        @pl.when(i > 1)
+        def _():
+            gate_copy(i - 1).start()
+
         return 0
 
-    lax.fori_loop(0, shards, gate_step, 0)
+    lax.fori_loop(1, shards, gate_step, 0)
+    gate_in[me] = dot(picked(place, slot, me, per, 0, width), gate_ref[...]).astype(BF16)
+    gate_copy(shards - 1).start()
     each(1, shards, lambda i: small_copy(i).wait())
     each(1, peers, lambda i: tail_copy(i).start())
     each(1, peers, lambda i: tail_copy(i).wait())
-    each(1, shards, lambda i: x_copy(i).wait())
-
-
-def move_rows(place, xs, small, gate, width, heads):
-    shards, peers = lax.axis_size("seq"), lax.axis_size("head")
-    rows, inner = xs.shape
-    per = rows // shards
-    vmem = pl.BlockSpec(memory_space=pltpu.VMEM)
-    return pl.pallas_call(
-        functools.partial(move_kernel, width, heads),
-        in_specs=[vmem] * 4,
-        out_specs=[vmem] * 3,
-        out_shape=[
-            jax.ShapeDtypeStruct((shards, per + RIM, inner), BF16),
-            jax.ShapeDtypeStruct((peers, shards, per + RIM, LANES), BF16),
-            jax.ShapeDtypeStruct((shards, per, inner), BF16),
-        ],
-        scratch_shapes=[
-            pltpu.VMEM((shards, per + RIM, inner), BF16),
-            pltpu.VMEM((shards, per + RIM, LANES), BF16),
-            pltpu.SemaphoreType.DMA((2, shards)),
-            pltpu.SemaphoreType.DMA((2, shards)),
-            pltpu.SemaphoreType.DMA((2, peers)),
-        ],
-        compiler_params=pltpu.CompilerParams(
-            collective_id=0, has_side_effects=True, vmem_limit_bytes=56 << 20
-        ),
-    )(place, xs, small, gate)
-
-
-def doc_at(start_ref, position):
-    total = jnp.where(start_ref[0] <= position, 1, 0)
-    for j in range(1, start_ref.shape[0] - 1):
-        total = total + jnp.where(start_ref[j] <= position, 1, 0)
+
+
+def doc_at(starts, position):
+    total = jnp.where(starts[0] <= position, 1, 0)
+    for start in starts[1:]:
+        total = total + jnp.where(start <= position, 1, 0)
     return total
 
 
+def starts_of(length_ref):
+    starts = [jnp.int32(0)]
+    for j in range(length_ref.shape[0] - 1):
+        starts.append(starts[-1] + length_ref[j])
+    return starts
+
+
+def head_row(ref):
+    lane = iota((8, LANES), 1)
+    row = jnp.zeros((8, LANES), F32)
+    for head in range(ref.shape[0]):
+        row = jnp.where(lane == head, ref[head], row)
+    return row
+
+
 def scan_step(
-    chunk, chunks, per, heads, start_ref, arrived_ref, bc_ref, tail_ref, taps_ref, head_ref,
-    skip_ref, y_ref, query_ref, carry_ref, slot_ref, state_ref, total_ref,
+    chunk, base, heads, length_ref, arrived_ref, bc_ref, tail_ref, conv_x_ref, conv_bc_ref,
+    a_log_ref, dt_bias_ref, d_skip_ref,
+    y_ref, query_ref, carry_ref, slot_ref, state_ref, total_ref,
 ):
-    width = taps_ref.shape[0]
+    width = conv_x_ref.shape[0]
     inner = y_ref.shape[1]
     head_dim = inner // heads
-    rows_in = arrived_ref.shape[0]
-    base = start_ref[start_ref.shape[0] - 1]
+    rows_in = bc_ref.shape[0]
+    starts = starts_of(length_ref)
     origin = base + chunk * BLOCK
     here = pl.ds(pl.multiple_of(chunk * BLOCK, BLOCK), BLOCK)
 
     wanted = iota((BLOCK + RIM, rows_in), 0) + (chunk * BLOCK - RIM)
     pick = (wanted == slot_ref[0:1, :]).astype(F32).astype(BF16)
     column = iota((BLOCK, 1), 0) + origin
-    docs = doc_at(start_ref, column)
+    docs = doc_at(starts, column)
     matches = [None] + [
-        (doc_at(start_ref, column - lag) == docs) & (column >= lag) for lag in range(1, width)
+        (doc_at(starts, column - lag) == docs) & (column >= lag) for lag in range(1, width)
     ]
 
-    def convolved(packed, first):
-        count = packed.shape[1]
-        total = taps_ref[0:1, first : first + count] * packed[RIM:, :]
+    def convolved(packed, taps_ref):
+        total = taps_ref[0:1, :] * packed[RIM:, :]
         for lag in range(1, width):
-            part = taps_ref[lag : lag + 1, first : first + count] * packed[RIM - lag : RIM - lag + BLOCK, :]
+            part = taps_ref[lag : lag + 1, :] * packed[RIM - lag : RIM - lag + BLOCK, :]
             total = total + jnp.where(matches[lag], part, 0.0)
         return (total * jax.nn.sigmoid(total)).astype(BF16)
 
-    x = convolved(dot(pick, arrived_ref[...]), 0)
-    both = convolved(dot(pick, bc_ref[...]), inner)
+    x = convolved(dot(pick, arrived_ref[...].reshape(rows_in, inner)), conv_x_ref)
+    both = convolved(dot(pick, bc_ref[...]), conv_bc_ref)
     keys, query = both[:, :LANES], both[:, LANES:]
     query_ref[here, :] = query
     raw = dot(pick, tail_ref[...])[RIM:, :]
-    raw = raw + head_ref[1:2, :]
+    raw = raw + head_row(dt_bias_ref)[0:1, :]
     lane = iota((1, LANES), 1)
     step = jnp.maximum(raw, 0.0) + jnp.log1p(jnp.exp(-jnp.abs(raw)))
     step = jnp.where(lane < heads, step, 0.0)
-    rate = jnp.exp(head_ref[0:1, :])
+    rate = jnp.exp(head_row(a_log_ref)[0:1, :])
     decay = -rate * step
     lower = iota((BLOCK, BLOCK), 0) >= iota((BLOCK, BLOCK), 1)
     sums = jnp.dot(lower.astype(F32), decay, precision=HIGHEST, preferred_element_type=F32)
     sums_t = sums.T
     step_t = step.T
-    docs_row = doc_at(start_ref, iota((1, BLOCK), 1) + origin)
+    docs_row = doc_at(starts, iota((1, BLOCK), 1) + origin)
     linked = lower & (docs == docs_row)
     scores = jnp.where(linked, dot(query, keys, ((1,), (1,))), 0.0)
-    doc_before = doc_at(start_ref, origin - 1)
+    doc_before = doc_at(starts, origin - 1)
     doc_before = jnp.where(origin > 0, doc_before, 0)
-    doc_base = jnp.where(base > 0, doc_at(start_ref, base - 1), 0)
-    doc_last = doc_at(start_ref, origin + BLOCK - 1)
+    doc_base = jnp.where(base > 0, doc_at(starts, base - 1), 0)
+    doc_last = doc_at(starts, origin + BLOCK - 1)
     carried = jnp.where(docs == doc_before, jnp.exp(sums), 0.0)
     last = sums[BLOCK - 1 : BLOCK, :]
     closing = jnp.where(docs == doc_last, jnp.exp(jnp.minimum(last - sums, 0.0)), 0.0) * step
@@ -267,7 +262,8 @@
     carried_all = expanded(carried, heads, head_dim, inner)
     state = state_ref[...]
     x32 = x.astype(F32)
-    y_ref[here, :] = carried_all * dot_right(query, state) + skip_ref[0:1, :] * x32
+    skip = expanded(head_row(d_skip_ref), heads, head_dim, inner)[0:1, :]
+    y_ref[here, :] = carried_all * dot_right(query, state) + skip * x32
     weighted = expanded(closing, heads, head_dim, inner) * x32
     state_ref[...] = carried_all[BLOCK - 1 : BLOCK, :] * state + dot_turned(keys, weighted)
 
@@ -291,16 +287,16 @@
     within = iota((8, shards * block), 1) % block
     slot_ref[...] = jnp.where(within >= per, place - per * shards, place)
     for source in range(shards):
-        gate_slot_ref[:, source * per : (source + 1) * per] = place[
-            :, source * block : source * block + per
-        ]
+        gate_slot_ref[source] = place[:, source * block : source * block + per]
 
 
 def layer_kernel(
-    per, heads, full_inner, start_ref, arrived_ref, bc_ref, tail_ref, taps_ref, head_ref, skip_ref,
-    gain_ref, gate_ref, out_ref,
-    y_ref, query_ref, carry_ref, slot_ref, gate_slot_ref, state_ref, total_ref,
-    gate_in, came, onward, incoming, squares, gate_sems, own_sem, state_sems, square_sems,
+    per, heads, full_inner, length_ref, a_log_ref, dt_bias_ref, d_skip_ref, place_ref, x_ref,
+    small_ref, gate_ref, conv_x_ref, conv_bc_ref, gain_ref, out_ref,
+    arrived_ref, tails_ref, x_send, small_send, gate_send, bc_ref, tail_ref,
+    y_ref, gate_sum, query_ref, carry_ref, slot_ref, gate_slot_ref, state_ref, total_ref,
+    gate_in, came, onward, incoming, squares,
+    x_sems, small_sems, tail_sems, gate_sems, state_sems, square_sems,
 ):
     shards, peers = lax.axis_size("seq"), lax.axis_size("head")
     me, own = lax.axis_index("seq"), lax.axis_index("head")
@@ -309,15 +305,14 @@
     chunks = rows // BLOCK
     head_dim = inner // heads
     pieces, _, wide = came.shape
+    width = conv_x_ref.shape[0]
+    block = per + RIM
+    quarter = bc_ref.shape[1] // peers
 
     def gate_copy(i):
-        to = lax.rem(me + i, shards)
         return remote(
-            gate_ref.at[to], gate_in.at[me], gate_sems.at[0, i], gate_sems.at[1, i], "seq", i
-        )
-
-    def own_copy():
-        return pltpu.make_async_copy(gate_ref.at[me], gate_in.at[me], own_sem)
+            gate_send.at[i], gate_in.at[me], gate_sems.at[0, i], gate_sems.at[1, i], "seq", i
+        )
 
     def state_copy(piece):
         return remote(
@@ -330,27 +325,34 @@
             square_sems.at[0, chunk, i], square_sems.at[1, chunk, i], "head", i,
         )
 
-    def each(first, last, action):
-        def once(i, _):
-            action(i)
-            return 0
-
-        lax.fori_loop(first, last, once, 0)
-
     @pl.when(step == 0)
     def _():
-        greet(("seq", "head"))
-        each(1, shards, lambda i: gate_copy(i).start())
-        own_copy().start()
+        move_step(
+            width, heads, place_ref, x_ref, small_ref, gate_ref, arrived_ref, tails_ref, gate_in,
+            x_send, small_send, gate_send, x_sems, small_sems, tail_sems, gate_copy,
+        )
+        for source in range(shards):
+            here = slice(source * block, (source + 1) * block)
+            parts = [tails_ref[peer, source][:, LANES - quarter :] for peer in range(peers)]
+            bc_ref[here, :] = jnp.concatenate(parts, 1)
+            tail_ref[here, :] = tails_ref[own, source]
         start_step(per, heads, tail_ref, slot_ref, gate_slot_ref)
         state_ref[...] = jnp.zeros_like(state_ref)
         total_ref[...] = jnp.zeros_like(total_ref)
+        each(
+            1,
+            shards,
+            lambda i: remote(
+                x_send.at[i], arrived_ref.at[me], x_sems.at[0, i], x_sems.at[1, i], "seq", i
+            ).wait(),
+        )
 
     @pl.when(step < chunks)
     def _():
         scan_step(
-            step, chunks, per, heads, start_ref, arrived_ref, bc_ref, tail_ref, taps_ref, head_ref,
-            skip_ref, y_ref, query_ref, carry_ref, slot_ref, state_ref, total_ref,
+            step, me * rows, heads, length_ref, arrived_ref, bc_ref, tail_ref, conv_x_ref,
+            conv_bc_ref, a_log_ref, dt_bias_ref, d_skip_ref,
+            y_ref, query_ref, carry_ref, slot_ref, state_ref, total_ref,
         )
 
     @pl.when(step == chunks - 1)
@@ -385,8 +387,32 @@
             for piece in range(pieces):
                 state_copy(piece).wait_send()
 
-        each(1, shards, lambda i: gate_copy(i).wait())
-        own_copy().wait()
+        def add_state(chunk):
+            here = pl.ds(pl.multiple_of(chunk * BLOCK, BLOCK), BLOCK)
+            carried = expanded(carry_ref[here, :], heads, head_dim, inner)
+            y_ref[here, :] += carried * dot(query_ref[here, :], state_ref[...].astype(BF16))
+
+        each(0, chunks, add_state)
+
+        def unsort(i, fresh):
+            source = lax.rem(me - i + shards, shards)
+
+            def one(chunk):
+                here = pl.ds(pl.multiple_of(chunk * BLOCK, BLOCK), BLOCK)
+                wanted = iota((BLOCK, per), 0) + chunk * BLOCK
+                pick = (wanted == gate_slot_ref[source, 0:1, :]).astype(F32).astype(BF16)
+                part = dot(pick, gate_in[source])
+                gate_sum[here, :] = part if fresh else gate_sum[here, :] + part
+
+            each(0, chunks, one)
+
+        unsort(0, True)
+
+        def unsort_next(i):
+            gate_copy(i).wait()
+            unsort(i, False)
+
+        each(1, shards, unsort_next)
 
     @pl.when((step > chunks) & (step <= 2 * chunks))
     def _():
@@ -396,11 +422,8 @@
     def _():
         chunk = step - chunks
         here = pl.ds(pl.multiple_of(chunk * BLOCK, BLOCK), BLOCK)
-        wanted = iota((BLOCK, rows), 0) + chunk * BLOCK
-        pick = (wanted == gate_slot_ref[0:1, :]).astype(F32).astype(BF16)
-        gate = dot(pick, gate_in[...].reshape(rows, inner))
-        carried = expanded(carry_ref[here, :], heads, head_dim, inner)
-        y = y_ref[here, :] + carried * dot(query_ref[here, :], state_ref[...].astype(BF16))
+        gate = gate_sum[here, :]
+        y = y_ref[here, :]
         gated = y * (gate * jax.nn.sigmoid(gate))
         y_ref[here, :] = gated
         total = jnp.sum(gated * gated, axis=1, keepdims=True)
@@ -419,75 +442,69 @@
         out_ref[...] = (y_ref[here, :] * scale * gain_ref[0:1, :]).astype(BF16)
 
 
-def layer(starts, arrived, bc, tail, taps, head_rows, skip, gain, gate, per, heads, rows, full_inner):
+def layer(lengths, a_log, dt_bias, d_skip, place, xs, small, gate, conv_x, conv_bc, gain, full_inner):
     shards, peers = lax.axis_size("seq"), lax.axis_size("head")
-    rows_in, inner = arrived.shape
+    rows, inner = xs.shape
+    heads = a_log.shape[0]
+    per = rows // shards
+    block = per + RIM
     chunks = rows // BLOCK
     wide = 2 * LANES
+    pieces = inner // wide
     vmem = pl.BlockSpec(memory_space=pltpu.VMEM)
     return pl.pallas_call(
         functools.partial(layer_kernel, per, heads, full_inner),
         grid=(3 * chunks,),
-        in_specs=[pl.BlockSpec(memory_space=pltpu.SMEM)]
-        + [vmem] * 7
-        + [pl.BlockSpec(memory_space=pl.ANY)],
+        in_specs=[pl.BlockSpec(memory_space=pltpu.SMEM)] * 4 + [vmem] * 7,
         out_specs=pl.BlockSpec((BLOCK, inner), lambda k: (jnp.maximum(k - 2 * chunks, 0), 0)),
         out_shape=jax.ShapeDtypeStruct((rows, inner), BF16),
         scratch_shapes=[
+            pltpu.VMEM((shards, block, inner), BF16),
+            pltpu.VMEM((peers, shards, block, LANES), BF16),
+            pltpu.VMEM((shards, block, inner), BF16),
+            pltpu.VMEM((shards, block, LANES), BF16),
+            pltpu.VMEM((shards, per, inner), BF16),
+            pltpu.VMEM((shards * block, conv_bc.shape[1]), BF16),
+            pltpu.VMEM((shards * block, LANES), BF16),
+            pltpu.VMEM((rows, inner), F32),
             pltpu.VMEM((rows, inner), F32),
             pltpu.VMEM((rows, LANES), BF16),
             pltpu.VMEM((rows, LANES), F32),
-            pltpu.VMEM((8, rows_in), jnp.int32),
-            pltpu.VMEM((8, rows), jnp.int32),
+            pltpu.VMEM((8, shards * block), jnp.int32),
+            pltpu.VMEM((shards, 8, per), jnp.int32),
             pltpu.VMEM((LANES, inner), F32),
             pltpu.VMEM((8, LANES), F32),
             pltpu.VMEM((shards, per, inner), BF16),
-            pltpu.VMEM((inner // wide, LANES, wide), BF16),
-            pltpu.VMEM((inner // wide, LANES, wide), BF16),
+            pltpu.VMEM((pieces, LANES, wide), BF16),
+            pltpu.VMEM((pieces, LANES, wide), BF16),
             pltpu.VMEM((LANES, inner), F32),
             pltpu.VMEM((peers, chunks, 8, BLOCK), F32),
             pltpu.SemaphoreType.DMA((2, shards)),
-            pltpu.SemaphoreType.DMA,
-            pltpu.SemaphoreType.DMA((2, inner // wide)),
+            pltpu.SemaphoreType.DMA((2, shards)),
+            pltpu.SemaphoreType.DMA((2, peers)),
+            pltpu.SemaphoreType.DMA((2, shards)),
+            pltpu.SemaphoreType.DMA((2, pieces)),
             pltpu.SemaphoreType.DMA((2, chunks, peers)),
         ],
         compiler_params=pltpu.CompilerParams(
-            collective_id=1, has_side_effects=True, vmem_limit_bytes=60 << 20
+            collective_id=0, has_side_effects=True, vmem_limit_bytes=60 << 20
         ),
-    )(starts, arrived, bc, tail, taps, head_rows, skip, gain, gate)
+    )(lengths, a_log, dt_bias, d_skip, place, xs, small, gate, conv_x, conv_bc, gain)
 
 
 def body(
     xs, gate_in, bc_in, dt_in, placement, lengths,
     conv_x, conv_bc, a_log, dt_bias, d_skip, norm_gain, *, full_inner,
 ):
-    shards = lax.axis_size("seq")
-    mine = lax.axis_index("seq")
-    rows, inner = xs.shape
+    rows = xs.shape[0]
     heads = a_log.shape[0]
-    head_dim = inner // heads
-    per = rows // shards
-    width = conv_x.shape[0]
-    place = placement[None, :]
     quarter = bc_in.shape[1] // lax.axis_size("head")
     bc_own = lax.dynamic_slice_in_dim(bc_in, lax.axis_index("head") * quarter, quarter, 1)
     spare = jnp.zeros((rows, LANES - heads - quarter), BF16)
     small = jnp.concatenate([dt_in, spare, bc_own], 1)
-
-    arrived, tails, gate = move_rows(place, xs, small, gate_in, width, heads)
-    tails = tails.reshape(tails.shape[0], -1, LANES)
-    bc = tails[:, :, LANES - quarter :].transpose(1, 0, 2).reshape(tails.shape[1], -1)
-    starts = jnp.concatenate(
-        [jnp.cumsum(lengths) - lengths, jnp.asarray(mine * rows, jnp.int32)[None]]
-    )
-    taps = jnp.concatenate([conv_x, conv_bc], 1)
-    head_rows = jnp.zeros((8, LANES), F32).at[0, :heads].set(a_log).at[1, :heads].set(dt_bias)
-    skip = jnp.broadcast_to(jnp.repeat(d_skip, head_dim)[None, :], (8, inner))
-    gain = jnp.broadcast_to(norm_gain[None, :], (8, inner))
-    tail = lax.dynamic_index_in_dim(tails, lax.axis_index("head"), 0, keepdims=False)
     return layer(
-        starts, arrived.reshape(shards * (per + RIM), inner), bc, tail, taps, head_rows, skip,
-        gain, gate, per, heads, rows, full_inner,
+        lengths, a_log, dt_bias, d_skip, placement[None, :], xs, small, gate_in, conv_x, conv_bc,
+        norm_gain[None, :], full_inner,
     )
 
 

time: 178 us -> 163 us (0.916)
  local copies, waits for them, and re-layouts: 13.6 us -> 5.89 us
  other arithmetic: 4.34 us -> 0.87 us
  Pallas kernels: 159 us -> 156 us
    pallas_call x1 -> x0, Pallas kernels: 74.7 us -> none  [move_rows(): pl.pallas_call(functools.partial(move_kernel, width, heads), in_specs=[vm...]
    pallas_call x1, Pallas kernels: 84.7 us -> 156 us  [layer(): pl.pallas_call(functools.partial(layer_kernel, per, heads, full_inner), g...]
    concatenate x2 -> x0, other arithmetic: 1.93 us -> none  [the longest x1 1.37 us: body(): taps = jnp.concatenate([conv_x, conv_bc], 1)]
    unnamed x7 -> x4, local copies, waits for them, and re-layouts: 4.94 us -> 4.33 us
where the time goes in v3:
time: 163 us
  Pallas kernels  156 us (96%)
  local copies, waits for them, and re-layouts  5.89 us (4%)
    pallas_call x1, Pallas kernels, layer(): pl.pallas_call(functools.partial(layer_kernel, per, heads, full_inner), g...  156 us
    unnamed x4, local copies, waits for them, and re-layouts  4.33 us

profile of v3, /device:TPU:25, one launch (start us, length us, event | category | flops | bytes accessed | tf_op | source)
XLA Modules:
  0.0 162.6 jit_solution(14874153517357258562)
XLA Ops:
  0.0 0.0 copy-start
  0.0 0.1 pad.1.clone
  0.1 1.3 broadcast_in_dim.11.gain_ref
  1.4 0.0 copy-done
  1.4 0.1 constant_dynamic-slice_fusion
  1.6 0.9 copy.13
  2.5 0.9 pad_maximum_fusion.small_ref
  3.4 155.8 %shard_map.118 = bf16[1024,1280]{1,0:T(8,128)(2,1)} custom-call(s32[3]{0:T(128)} %length_ref.1, f32[16]{0:T(128)} %a_log_ref.1, f32[16]{0:T(128)} %dt_bias_ref.1, f32[16]{0:T(128)} %d_skip_ref.1, s32[1,1024]{1,0:T(1,128)} %bitcast.1, bf16[1024,1280]{1,0:T(8,128)(2,1)} %x_ref.1, bf16[1024,128]{1,0:T(8,128)(2,1)} %pad_maximum_fusion.small_ref, ...), custom_call_target="tpu_custom_call" | custom-call | tf_op jit(solution)/shard_map/pallas_call | solution.py:455
  159.2 3.4 %copy.15 = bf16[1024,1280]{1,0:T(8,128)(2,1)} copy(bf16[1024,1280]{1,0:T(8,128)(2,1)} %shard_map.118) | data formatting | bytes 5242880
  (1 shorter events, 0.0 us)
Async XLA Ops:
  0.0 1.4 copy-start
